TPU v7x, 128 devices: a whole 4x4x4 slice. The times are simulated.
128 devices in a mesh: leaf: 16 (over y, x), front: 8 (over z, core).
Axes of the slice: x: 4, y: 4, z: 4, core: 2. Of those that a mesh axis runs over, the one named last changes fastest.
Arguments:
- rhs: bfloat16 [3, 16384, 256], P(None, ('leaf', 'front')), may hold values from -6 to 6
- inverse_blocks: bfloat16 [16384, 7168], P(('leaf', 'front')), may hold values from -0.125 to 0.125
- update_blocks: bfloat16 [16384, 3072], P(('leaf', 'front')), may hold values from -0.125 to 0.125
- asm_owner: int32 [2, 16384, 1], P(None, ('leaf', 'front')), may hold values from 0 to 15; in each aligned block of 128 rows (0 to 127, 128 to 255, ..., all dimensions but the last counted through in order) at most 32 rows name the same one
- asm_row: int32 [2, 16384], P(None, ('leaf', 'front')), may hold values from 0 to 127
Outputs:
- solutions: float32 [3, 16384, 256], P(None, ('leaf', 'front'))
Inputs may be any that keep to these rules, and one draw needn't show every extreme that they name: `asm_owner`: among the 128 update rows of one device at one level (aligned blocks of rows), at most 32 name the same owner, and some block reaches 32.
All inputs are finite; a program needn't handle non-finite values.
Results may differ from a plain program's by a relative error of at most 0.03.
Values may be sent and summed in bfloat16 or wider, within the bound.
A program may use at most 64 MiB of HBM per device.

v0:
```python
import jax
import jax.numpy as jnp
from jax import lax
from jax.sharding import PartitionSpec as P

LEVELS = 3


def swapped(shard, axis, distance):
    return lax.ppermute(shard, axis, [(i, i ^ 1 << distance) for i in range(lax.axis_size(axis))])


def contract_rows(left, right):
    return lax.dot_general(
        left, right, (((0,), (0,)), ((), ())), preferred_element_type=jnp.float32
    )


def shards(rhs, inverse_blocks, update_blocks, asm_owner, asm_row):
    own_rows = rhs.shape[1]
    rhs_cols = rhs.shape[2]
    front_count = lax.axis_size("front")
    leaf_rows = front_count * own_rows
    leaf_id = lax.axis_index("leaf")

    def side_of(bit_index):
        return leaf_id // (1 << bit_index) % 2

    def node_gather(local, pair_bits):
        gathered = lax.all_gather(local, "front", axis=0, tiled=True)
        for bit_index in pair_bits:
            partner = swapped(gathered, "leaf", bit_index)
            gathered = jnp.where(
                side_of(bit_index) == 1,
                jnp.concatenate([partner, gathered], 0),
                jnp.concatenate([gathered, partner], 0),
            )
        return gathered

    def node_reduce(partial_value, pair_bits):
        for bit_index in pair_bits:
            half_rows = partial_value.shape[0] // 2
            upper_half = side_of(bit_index) == 1
            kept = jnp.where(upper_half, partial_value[half_rows:], partial_value[:half_rows])
            handed = jnp.where(upper_half, partial_value[:half_rows], partial_value[half_rows:])
            partial_value = kept + swapped(handed.astype(jnp.bfloat16), "leaf", bit_index).astype(
                handed.dtype
            )
        partial_value = lax.psum_scatter(
            partial_value.astype(jnp.bfloat16), "front", scatter_dimension=0, tiled=True
        ).astype(jnp.float32)
        return partial_value

    assembled = jnp.zeros((own_rows, rhs_cols), jnp.float32)
    solved_all = []
    records = []
    for level_index in range(LEVELS):
        front_rows = leaf_rows << level_index
        column_start = leaf_rows * ((1 << level_index) - 1)
        pair_bits = list(range(level_index))
        pivot_rhs = (rhs[level_index].astype(jnp.float32) - assembled).astype(jnp.bfloat16)
        pivot_node = node_gather(pivot_rhs, pair_bits)
        solved = jnp.dot(
            inverse_blocks[:, column_start : column_start + front_rows],
            pivot_node,
            preferred_element_type=jnp.float32,
        ).astype(jnp.bfloat16)
        solved_all.append(solved)
        if level_index + 1 < LEVELS:
            solved_node = node_gather(solved, pair_bits)
            update = jnp.dot(
                update_blocks[:, column_start : column_start + front_rows],
                solved_node,
                preferred_element_type=jnp.float32,
            ).astype(jnp.bfloat16)
            owner_ids = asm_owner[level_index, :, 0]
            parent_row = asm_row[level_index]
            target_local = owner_ids * own_rows + parent_row
            selector = (target_local[:, None] == jnp.arange(2 * leaf_rows)[None, :]).astype(
                jnp.bfloat16
            )
            records.append(selector)
            assembled = node_reduce(contract_rows(selector, update), [level_index])
    solutions = [None] * LEVELS
    below = None
    for level_index in reversed(range(LEVELS)):
        front_rows = leaf_rows << level_index
        column_start = leaf_rows * ((1 << level_index) - 1)
        down_bits = list(reversed(range(level_index)))
        if level_index + 1 == LEVELS:
            weights = solved_all[level_index]
        else:
            pair_block = node_gather(below, [level_index])
            fetched = jnp.dot(
                records[level_index], pair_block, preferred_element_type=jnp.float32
            ).astype(jnp.bfloat16)
            carried = node_reduce(
                contract_rows(update_blocks[:, column_start : column_start + front_rows], fetched),
                down_bits,
            )
            weights = (solved_all[level_index].astype(jnp.float32) - carried).astype(jnp.bfloat16)
        solution = node_reduce(
            contract_rows(inverse_blocks[:, column_start : column_start + front_rows], weights),
            down_bits,
        )
        solutions[level_index] = solution
        below = solution.astype(jnp.bfloat16)
    return jnp.stack(solutions)


def solution(mesh):
    placed = (
        P(None, ("leaf", "front"), None),
        P(("leaf", "front"), None),
        P(("leaf", "front"), None),
        P(None, ("leaf", "front"), None),
        P(None, ("leaf", "front")),
    )
    return jax.shard_map(
        shards,
        mesh=mesh,
        in_specs=placed,
        out_specs=P(None, ("leaf", "front"), None),
        check_vma=False,
    )
```

profile of v0, /device:TPU:1, one launch (start us, length us, event | category | flops | bytes accessed | tf_op | source)
XLA Modules:
  0.0 548.9 jit_solution(4075228296773122472)
XLA Ops:
  7.4 15.6 %all-gather = bf16[1,1024,256]{2,1,0:T(8,128)(2,1)S(1)} all-gather(bf16[1,128,256]{2,1,0:T(8,128)(2,1)S(1)} %slice.90), channel_id=2, replica_groups=mesh['leaf'=16,'front'=8] {'front'}, dimensions={1}, use_global_device_ids=true | all-gather | bytes 589824 | tf_op jit(solution)/shard_map/all_gather | solution.py:30
  24.2 13.1 %all_gather.22 = bf16[1024,256]{1,0:T(8,128)(2,1)S(1)} all-gather(bf16[128,256]{1,0:T(8,128)(2,1)S(1)} %convolution_convert_fusion.7), channel_id=1, replica_groups=mesh['leaf'=16,'front'=8] {'front'}, dimensions={0}, use_global_device_ids=true | all-gather | bytes 589824 | tf_op jit(solution)/shard_map/all_gather | solution.py:30
  40.7 12.2 %collective-permute-done = bf16[1024,256]{1,0:T(8,128)(2,1)S(1)} collective-permute-done((bf16[1024,256]{1,0:T(8,128)(2,1)S(1)}, bf16[1024,256]{1,0:T(8,128)(2,1)S(1)}, u32[]{:S(2)}, u32[]{:S(2)}) %collective-permute-start) | collective-permute-done | bytes 524320 | tf_op jit(solution)/shard_map/ppermute | solution.py:10
  53.9 29.8 %reduce-scatter.8.cloned.1.call-done = bf16[128,256]{1,0:T(8,128)(2,1)} async-done(((bf16[1024,256]{1,0:T(8,128)(2,1)}), bf16[128,256]{1,0:T(8,128)(2,1)}) %reduce-scatter.8.cloned.1.call-update) | async-done | bytes 65552 | tf_op jit(solution)/shard_map/reduce_scatter | solution.py:49
  84.6 16.5 %all_gather.23 = bf16[1024,256]{1,0:T(8,128)(2,1)S(1)} all-gather(bf16[128,256]{1,0:T(8,128)(2,1)S(1)} %fusion.79), channel_id=1, replica_groups=mesh['leaf'=16,'front'=8] {'front'}, dimensions={0}, use_global_device_ids=true | all-gather | bytes 589824 | tf_op jit(solution)/shard_map/all_gather | solution.py:30
  102.3 12.2 %collective-permute-done.1 = bf16[1024,256]{1,0:T(8,128)(2,1)S(1)} collective-permute-done((bf16[1024,256]{1,0:T(8,128)(2,1)S(1)}, bf16[1024,256]{1,0:T(8,128)(2,1)S(1)}, u32[]{:S(2)}, u32[]{:S(2)}) %collective-permute-start.1) | collective-permute-done | bytes 524320 | tf_op jit(solution)/shard_map/ppermute | solution.py:10
  115.9 13.9 %all_gather.24 = bf16[1024,256]{1,0:T(8,128)(2,1)S(1)} all-gather(bf16[128,256]{1,0:T(8,128)(2,1)S(1)} %fusion.11), channel_id=1, replica_groups=mesh['leaf'=16,'front'=8] {'front'}, dimensions={0}, use_global_device_ids=true | all-gather | bytes 589824 | tf_op jit(solution)/shard_map/all_gather | solution.py:30
  131.0 12.2 %collective-permute-done.2 = bf16[1024,256]{1,0:T(8,128)(2,1)S(1)} collective-permute-done((bf16[1024,256]{1,0:T(8,128)(2,1)S(1)}, bf16[1024,256]{1,0:T(8,128)(2,1)S(1)}, u32[]{:S(2)}, u32[]{:S(2)}) %collective-permute-start.2) | collective-permute-done | bytes 524320 | tf_op jit(solution)/shard_map/ppermute | solution.py:10
  148.5 11.2 %collective-permute-done.3 = bf16[1024,256]{1,0:T(8,128)(2,1)S(1)} collective-permute-done((bf16[1024,256]{1,0:T(8,128)(2,1)S(1)}, bf16[1024,256]{1,0:T(8,128)(2,1)S(1)}, u32[]{:S(2)}, u32[]{:S(2)}) %collective-permute-start.3) | collective-permute-done | bytes 524320 | tf_op jit(solution)/shard_map/ppermute | solution.py:10
  160.8 29.2 %reduce-scatter.10.cloned.1.call-done = bf16[128,256]{1,0:T(8,128)(2,1)} async-done(((bf16[1024,256]{1,0:T(8,128)(2,1)}), bf16[128,256]{1,0:T(8,128)(2,1)}) %reduce-scatter.10.cloned.1.call-update) | async-done | bytes 65552 | tf_op jit(solution)/shard_map/reduce_scatter | solution.py:49
  190.9 16.6 %all_gather.25 = bf16[1024,256]{1,0:T(8,128)(2,1)S(1)} all-gather(bf16[128,256]{1,0:T(8,128)(2,1)S(1)} %fusion.78), channel_id=1, replica_groups=mesh['leaf'=16,'front'=8] {'front'}, dimensions={0}, use_global_device_ids=true | all-gather | bytes 589824 | tf_op jit(solution)/shard_map/all_gather | solution.py:30
  208.5 12.3 %collective-permute-done.4 = bf16[1024,256]{1,0:T(8,128)(2,1)S(1)} collective-permute-done((bf16[1024,256]{1,0:T(8,128)(2,1)S(1)}, bf16[1024,256]{1,0:T(8,128)(2,1)S(1)}, u32[]{:S(2)}, u32[]{:S(2)}) %collective-permute-start.4) | collective-permute-done | bytes 524320 | tf_op jit(solution)/shard_map/ppermute | solution.py:10
  223.8 22.7 %collective-permute-done.5 = bf16[2048,256]{1,0:T(8,128)(2,1)} collective-permute-done((bf16[2048,256]{1,0:T(8,128)(2,1)S(1)}, bf16[2048,256]{1,0:T(8,128)(2,1)}, u32[]{:S(2)}, u32[]{:S(2)}) %collective-permute-start.5) | collective-permute-done | bytes 1048608 | tf_op jit(solution)/shard_map/ppermute | solution.py:10
  257.5 21.7 %collective-permute-done.6 = bf16[2048,256]{1,0:T(8,128)(2,1)S(1)} collective-permute-done((bf16[2048,256]{1,0:T(8,128)(2,1)S(1)}, bf16[2048,256]{1,0:T(8,128)(2,1)S(1)}, u32[]{:S(2)}, u32[]{:S(2)}) %collective-permute-start.6) | collective-permute-done | bytes 1048608 | tf_op jit(solution)/shard_map/ppermute | solution.py:10
  293.7 30.8 %reduce-scatter.12.cloned.1.call-done = bf16[128,256]{1,0:T(8,128)(2,1)} async-done(((bf16[1024,256]{1,0:T(8,128)(2,1)}), bf16[128,256]{1,0:T(8,128)(2,1)}) %reduce-scatter.12.cloned.1.call-update) | async-done | bytes 65552 | tf_op jit(solution)/shard_map/reduce_scatter | solution.py:49
  324.5 16.9 %all_gather.26 = bf16[1024,256]{1,0:T(8,128)(2,1)S(1)} all-gather(bf16[128,256]{1,0:T(8,128)(2,1)} %reduce-scatter.12.cloned.1.call-done), channel_id=1, replica_groups=mesh['leaf'=16,'front'=8] {'front'}, dimensions={0}, use_global_device_ids=true | all-gather | bytes 589824 | tf_op jit(solution)/shard_map/all_gather | solution.py:30
  344.1 12.3 %collective-permute-done.8 = bf16[1024,256]{1,0:T(8,128)(2,1)} collective-permute-done((bf16[1024,256]{1,0:T(8,128)(2,1)S(1)}, bf16[1024,256]{1,0:T(8,128)(2,1)}, u32[]{:S(2)}, u32[]{:S(2)}) %collective-permute-start.8) | collective-permute-done | bytes 524320 | tf_op jit(solution)/shard_map/ppermute | solution.py:10
  360.1 11.3 %collective-permute-done.9 = bf16[1024,256]{1,0:T(8,128)(2,1)S(1)} collective-permute-done((bf16[1024,256]{1,0:T(8,128)(2,1)S(1)}, bf16[1024,256]{1,0:T(8,128)(2,1)S(1)}, u32[]{:S(2)}, u32[]{:S(2)}) %collective-permute-start.9) | collective-permute-done | bytes 524320 | tf_op jit(solution)/shard_map/ppermute | solution.py:10
  372.4 29.1 %reduce-scatter.14.cloned.1.call-done = bf16[128,256]{1,0:T(8,128)(2,1)} async-done(((bf16[1024,256]{1,0:T(8,128)(2,1)}), bf16[128,256]{1,0:T(8,128)(2,1)}) %reduce-scatter.14.cloned.1.call-update) | async-done | bytes 65552 | tf_op jit(solution)/shard_map/reduce_scatter | solution.py:49
  414.1 33.9 %reduce-scatter.16.cloned.1.call-done = bf16[128,256]{1,0:T(8,128)(2,1)} async-done(((bf16[1024,256]{1,0:T(8,128)(2,1)}), bf16[128,256]{1,0:T(8,128)(2,1)}) %reduce-scatter.16.cloned.1.call-update) | async-done | bytes 65552 | tf_op jit(solution)/shard_map/reduce_scatter | solution.py:49
  448.0 16.7 %all_gather.27 = bf16[1024,256]{1,0:T(8,128)(2,1)S(1)} all-gather(bf16[128,256]{1,0:T(8,128)(2,1)} %reduce-scatter.16.cloned.1.call-done), channel_id=1, replica_groups=mesh['leaf'=16,'front'=8] {'front'}, dimensions={0}, use_global_device_ids=true | all-gather | bytes 589824 | tf_op jit(solution)/shard_map/all_gather | solution.py:30
  466.0 12.1 %collective-permute-done.11 = bf16[1024,256]{1,0:T(8,128)(2,1)S(1)} collective-permute-done((bf16[1024,256]{1,0:T(8,128)(2,1)S(1)}, bf16[1024,256]{1,0:T(8,128)(2,1)S(1)}, u32[]{:S(2)}, u32[]{:S(2)}) %collective-permute-start.11) | collective-permute-done | bytes 524320 | tf_op jit(solution)/shard_map/ppermute | solution.py:10
  479.9 28.3 %reduce-scatter.18.cloned.1.call-done = bf16[128,256]{1,0:T(8,128)(2,1)} async-done(((bf16[1024,256]{1,0:T(8,128)(2,1)}), bf16[128,256]{1,0:T(8,128)(2,1)}) %reduce-scatter.18.cloned.1.call-update) | async-done | bytes 65552 | tf_op jit(solution)/shard_map/reduce_scatter | solution.py:49
  510.4 30.1 %reduce-scatter.20.cloned.1.call-done = bf16[128,256]{1,0:T(8,128)(2,1)} async-done(((bf16[1024,256]{1,0:T(8,128)(2,1)}), bf16[128,256]{1,0:T(8,128)(2,1)}) %reduce-scatter.20.cloned.1.call-update) | async-done | bytes 65552 | tf_op jit(solution)/shard_map/reduce_scatter | solution.py:49
  (69 shorter events, 74.7 us)
Async XLA Ops:
  6.5 77.2 %reduce-scatter.8.cloned.1.call-start = ((), (), s32[]{:S(2)}) async-start(), calls=%async_computation.7 | async-start | bytes 589824 | tf_op jit(solution)/shard_map/reduce_scatter | solution.py:49
  39.4 44.3 %copy-start.3 = (bf16[3,128,256]{2,1,0:T(8,128)(2,1)S(1)}, bf16[3,128,256]{2,1,0:T(8,128)(2,1)}, u32[]{:S(2)}) copy-start(bf16[3,128,256]{2,1,0:T(8,128)(2,1)} %param.5) | copy-start | bytes 589828
  39.4 13.5 %collective-permute-start = (bf16[1024,256]{1,0:T(8,128)(2,1)S(1)}, bf16[1024,256]{1,0:T(8,128)(2,1)S(1)}, u32[]{:S(2)}, u32[]{:S(2)}) collective-permute-start(bf16[1024,256]{1,0:T(8,128)(2,1)S(1)} %select_convert_fusion.5), channel_id=1, source_target_pairs={{0,8},{8,0},{16,24},{24,16},{32,40},{40,32},{48,56},{56,48},{64,72... | collective-permute-start | bytes 1572872 | tf_op jit(solution)/shard_map/ppermute | solution.py:10
  53.9 136.1 %reduce-scatter.10.cloned.1.call-start = ((), (), s32[]{:S(2)}) async-start(), calls=%async_computation.8 | async-start | bytes 589824 | tf_op jit(solution)/shard_map/reduce_scatter | solution.py:49
  101.1 13.4 %collective-permute-start.1 = (bf16[1024,256]{1,0:T(8,128)(2,1)S(1)}, bf16[1024,256]{1,0:T(8,128)(2,1)S(1)}, u32[]{:S(2)}, u32[]{:S(2)}) collective-permute-start(bf16[1024,256]{1,0:T(8,128)(2,1)S(1)} %all_gather.23), channel_id=1, source_target_pairs={{0,8},{8,0},{16,24},{24,16},{32,40},{40,32},{48,56},{56,48},{64,72... | collective-permute-start | bytes 1572872 | tf_op jit(solution)/shard_map/ppermute | solution.py:10
  129.8 13.4 %collective-permute-start.2 = (bf16[1024,256]{1,0:T(8,128)(2,1)S(1)}, bf16[1024,256]{1,0:T(8,128)(2,1)S(1)}, u32[]{:S(2)}, u32[]{:S(2)}) collective-permute-start(bf16[1024,256]{1,0:T(8,128)(2,1)S(1)} %all_gather.24), channel_id=1, source_target_pairs={{0,8},{8,0},{16,24},{24,16},{32,40},{40,32},{48,56},{56,48},{64,72... | collective-permute-start | bytes 1572872 | tf_op jit(solution)/shard_map/ppermute | solution.py:10
  145.7 14.0 %collective-permute-start.3 = (bf16[1024,256]{1,0:T(8,128)(2,1)S(1)}, bf16[1024,256]{1,0:T(8,128)(2,1)S(1)}, u32[]{:S(2)}, u32[]{:S(2)}) collective-permute-start(bf16[1024,256]{1,0:T(8,128)(2,1)S(1)} %select_convert_fusion.4), channel_id=1, source_target_pairs={{0,16},{8,24},{16,0},{24,8},{32,48},{40,56},{48,32},{56,40},{64,80... | collective-permute-start | bytes 1572872 | tf_op jit(solution)/shard_map/ppermute | solution.py:10
  160.8 85.7 %copy-start = (bf16[128,7168]{1,0:T(8,128)(2,1)S(1)}, bf16[128,7168]{1,0:T(8,128)(2,1)}, u32[]{:S(2)}) copy-start(bf16[128,7168]{1,0:T(8,128)(2,1)} %param.6) | copy-start | bytes 5505028
  160.8 163.7 %reduce-scatter.12.cloned.1.call-start = ((), (), s32[]{:S(2)}) async-start(), calls=%async_computation.9 | async-start | bytes 589824 | tf_op jit(solution)/shard_map/reduce_scatter | solution.py:49
  207.4 13.4 %collective-permute-start.4 = (bf16[1024,256]{1,0:T(8,128)(2,1)S(1)}, bf16[1024,256]{1,0:T(8,128)(2,1)S(1)}, u32[]{:S(2)}, u32[]{:S(2)}) collective-permute-start(bf16[1024,256]{1,0:T(8,128)(2,1)S(1)} %all_gather.25), channel_id=1, source_target_pairs={{0,8},{8,0},{16,24},{24,16},{32,40},{40,32},{48,56},{56,48},{64,72... | collective-permute-start | bytes 1572872 | tf_op jit(solution)/shard_map/ppermute | solution.py:10
  221.1 25.4 %collective-permute-start.5 = (bf16[2048,256]{1,0:T(8,128)(2,1)S(1)}, bf16[2048,256]{1,0:T(8,128)(2,1)}, u32[]{:S(2)}, u32[]{:S(2)}) collective-permute-start(bf16[2048,256]{1,0:T(8,128)(2,1)S(1)} %maximum_select_fusion.11), channel_id=1, source_target_pairs={{0,16},{8,24},{16,0},{24,8},{32,48},{40,56},{48,32},{56,40},{64,80... | collective-permute-start | bytes 3145736 | tf_op jit(solution)/shard_map/ppermute | solution.py:10
  254.8 24.4 %collective-permute-start.6 = (bf16[2048,256]{1,0:T(8,128)(2,1)S(1)}, bf16[2048,256]{1,0:T(8,128)(2,1)S(1)}, u32[]{:S(2)}, u32[]{:S(2)}) collective-permute-start(bf16[2048,256]{1,0:T(8,128)(2,1)S(1)} %select_convert_fusion), channel_id=1, source_target_pairs={{0,16},{8,24},{16,0},{24,8},{32,48},{40,56},{48,32},{56,40},{64,80... | collective-permute-start | bytes 3145736 | tf_op jit(solution)/shard_map/ppermute | solution.py:10
  281.9 74.5 %copy-start.4 = (bf16[128,3072]{1,0:T(8,128)(2,1)S(1)}, bf16[128,3072]{1,0:T(8,128)(2,1)}, u32[]{:S(2)}) copy-start(bf16[128,3072]{1,0:T(8,128)(2,1)} %param.7) | copy-start | bytes 2359300
  281.9 10.7 %collective-permute-start.7 = (bf16[1024,256]{1,0:T(8,128)(2,1)S(1)}, bf16[1024,256]{1,0:T(8,128)(2,1)S(1)}, u32[]{:S(2)}, u32[]{:S(2)}) collective-permute-start(bf16[1024,256]{1,0:T(8,128)(2,1)S(1)} %select_convert_fusion.3), channel_id=1, source_target_pairs={{0,8},{8,0},{16,24},{24,16},{32,40},{40,32},{48,56},{56,48},{64,72... | collective-permute-start | bytes 1572872 | tf_op jit(solution)/shard_map/ppermute | solution.py:10
  293.6 107.9 %reduce-scatter.14.cloned.1.call-start = ((), (), s32[]{:S(2)}) async-start(), calls=%async_computation.10 | async-start | bytes 589824 | tf_op jit(solution)/shard_map/reduce_scatter | solution.py:49
  341.4 15.0 %collective-permute-start.8 = (bf16[1024,256]{1,0:T(8,128)(2,1)S(1)}, bf16[1024,256]{1,0:T(8,128)(2,1)}, u32[]{:S(2)}, u32[]{:S(2)}) collective-permute-start(bf16[1024,256]{1,0:T(8,128)(2,1)S(1)} %all_gather.26), channel_id=1, source_target_pairs={{0,16},{8,24},{16,0},{24,8},{32,48},{40,56},{48,32},{56,40},{64,80... | collective-permute-start | bytes 1572872 | tf_op jit(solution)/shard_map/ppermute | solution.py:10
  358.8 12.5 %collective-permute-start.9 = (bf16[1024,256]{1,0:T(8,128)(2,1)S(1)}, bf16[1024,256]{1,0:T(8,128)(2,1)S(1)}, u32[]{:S(2)}, u32[]{:S(2)}) collective-permute-start(bf16[1024,256]{1,0:T(8,128)(2,1)S(1)} %select_convert_fusion.2), channel_id=1, source_target_pairs={{0,8},{8,0},{16,24},{24,16},{32,40},{40,32},{48,56},{56,48},{64,72... | collective-permute-start | bytes 1572872 | tf_op jit(solution)/shard_map/ppermute | solution.py:10
  372.4 75.6 %reduce-scatter.16.cloned.1.call-start = ((), (), s32[]{:S(2)}) async-start(), calls=%async_computation.11 | async-start | bytes 589824 | tf_op jit(solution)/shard_map/reduce_scatter | solution.py:49
  403.2 9.9 %collective-permute-start.10 = (bf16[1024,256]{1,0:T(8,128)(2,1)S(1)}, bf16[1024,256]{1,0:T(8,128)(2,1)S(1)}, u32[]{:S(2)}, u32[]{:S(2)}) collective-permute-start(bf16[1024,256]{1,0:T(8,128)(2,1)S(1)} %select_convert_fusion.1), channel_id=1, source_target_pairs={{0,8},{8,0},{16,24},{24,16},{32,40},{40,32},{48,56},{56,48},{64,72... | collective-permute-start | bytes 1572872 | tf_op jit(solution)/shard_map/ppermute | solution.py:10
  414.1 94.1 %reduce-scatter.18.cloned.1.call-start = ((), (), s32[]{:S(2)}) async-start(), calls=%async_computation.12 | async-start | bytes 589824 | tf_op jit(solution)/shard_map/reduce_scatter | solution.py:49
  464.7 75.7 %copy-start.1 = (bf16[128,256]{1,0:T(8,128)(2,1)S(1)}, bf16[128,256]{1,0:T(8,128)(2,1)}, u32[]{:S(2)}) copy-start(bf16[128,256]{1,0:T(8,128)(2,1)} %reduce-scatter.12.cloned.1.call-done) | copy-start | bytes 196612
  464.7 75.7 %copy-start.2 = (bf16[128,256]{1,0:T(8,128)(2,1)S(1)}, bf16[128,256]{1,0:T(8,128)(2,1)}, u32[]{:S(2)}) copy-start(bf16[128,256]{1,0:T(8,128)(2,1)} %reduce-scatter.16.cloned.1.call-done) | copy-start | bytes 196612
  464.7 13.4 %collective-permute-start.11 = (bf16[1024,256]{1,0:T(8,128)(2,1)S(1)}, bf16[1024,256]{1,0:T(8,128)(2,1)S(1)}, u32[]{:S(2)}, u32[]{:S(2)}) collective-permute-start(bf16[1024,256]{1,0:T(8,128)(2,1)S(1)} %all_gather.27), channel_id=1, source_target_pairs={{0,8},{8,0},{16,24},{24,16},{32,40},{40,32},{48,56},{56,48},{64,72... | collective-permute-start | bytes 1572872 | tf_op jit(solution)/shard_map/ppermute | solution.py:10
  479.9 60.6 %reduce-scatter.20.cloned.1.call-start = ((), (), s32[]{:S(2)}) async-start(), calls=%async_computation.13 | async-start | bytes 589824 | tf_op jit(solution)/shard_map/reduce_scatter | solution.py:49
  (2 other events, 61.6 us)
Sparse Core Ops, SparseCore 0:
  54.0 29.6 reduce-scatter.7
  160.9 29.0 reduce-scatter.9
  293.8 30.6 reduce-scatter.11
  372.5 28.9 reduce-scatter.13
  414.2 33.7 reduce-scatter.15
  480.0 28.1 reduce-scatter.17
  510.6 29.8 reduce-scatter.19
where the time goes:
time: 552 us; the launch traced here: 549 us
  waiting for transfers between devices  369 us (67%)
  blocking collectives  109 us (20%)
  starting transfers between devices  21 us (4%)
  matrix products  20.6 us (4%)
  other arithmetic  14.1 us (3%)
  between operations  13.6 us (2%)
    reduce_scatter x7, waiting for transfers between devices, node_reduce(): lax.psum_scatter(partial_value.astype(jnp.bfloat16), 'front', scatter_dim...  211 us
    ppermute x12, waiting for transfers between devices, swapped(): lax.ppermute(shard, axis, [(i, i ^ 1 << distance) for i in range(lax.axis...  158 us
    all_gather x7, blocking collectives, node_gather(): gathered = lax.all_gather(local, 'front', axis=0, tiled=True)  109 us
    ppermute x12, starting transfers between devices, swapped(): lax.ppermute(shard, axis, [(i, i ^ 1 << distance) for i in range(lax.axis...  20.8 us
    dot_general x7, matrix products, contract_rows(): lax.dot_general(left, right, (((0,), (0,)), ((), ())), preferred_element_...  18 us
  transfers between devices with their start and end apart: 19, of which 19 were waited for; matrix products, arithmetic and copies ran while one was open for 0% of the time, Pallas kernels for 0%

commit v1 on v0

v1 whole, which is shorter than its diff:
```python
import functools

import jax
import jax.numpy as jnp
from jax import lax
from jax.experimental import pallas as pl
from jax.experimental.pallas import tpu as pltpu
from jax.sharding import PartitionSpec as P

MESH = pl.DeviceIdType.MESH
F32, BF16 = jnp.float32, jnp.bfloat16

CHAINS = 2
ROW = 128
UNIT = 256
HALF = 128
NX, NZ = 4, 4
LEAF = UNIT * NZ
WIDTH = HALF // CHAINS
D_AT = (0, LEAF, 3 * LEAF)
E_AT = (0, LEAF)

Z_PEERS = (2, 1, 3)
PAIR_PEERS = ((1, 2), (1, 1), (1, 3), (0, 2), (1, 0), (0, 1), (0, 3))
QUAD_PEERS = tuple((dx, dz) for dx in (2, 1, 3, 0) for dz in (2, 1, 3, 0) if dx or dz)

CHAINED = (
    ("a0", 3), ("a1", 3), ("u0", 7), ("s1", 7), ("u1", 15), ("f1", 15), ("e1", 7), ("f0", 7), ("w0", 3), ("l0", 3),
    ("d2x", 3), ("d2z", 3), ("d1x", 1), ("d1z", 3),
)
SINGLE = (("core", 9), ("tz", 3), ("tx", 3), ("r1z", 3), ("r1x", 1), ("r2z", 3), ("r2x", 3), ("out", 3))
SEM_AT, SEM_COUNT = {}, 0
for _name, _n in CHAINED:
    SEM_AT[_name] = SEM_COUNT
    SEM_COUNT += _n * CHAINS
for _name, _n in SINGLE:
    SEM_AT[_name] = SEM_COUNT
    SEM_COUNT += _n


def nt(left, right):
    return lax.dot_general(left, right, (((1,), (1,)), ((), ())), preferred_element_type=F32)


def nn(left, right):
    return lax.dot_general(left, right, (((1,), (0,)), ((), ())), preferred_element_type=F32)


def kernel(
    owner_ref, row_ref, rhs_hbm, d_hbm, e_hbm, out_hbm,
    rhs_v, dm, em, m1, m2, swap, rt, tg, zr1, zr2, select,
    s0b, u0b, s1b, u1b, s2b, w1b,
    a0r, a1r, u0r, s1r, u1r, y1, y2,
    f1s, f1r, e1s, e1r, f0s, f0r, w0s, w0r, l0s, l0r,
    d2xs, d2xr, d2zs, d2zr, d1xs, d1xr, d1zs, d1zr,
    sol, stage_own, stage_other,
    ssem, rsem, lsem,
):
    leaf, front = lax.axis_index("leaf"), lax.axis_index("front")
    x, y = lax.rem(leaf, NX), leaf // NX
    z, c = front // 2, lax.rem(front, 2)
    other = 1 - c
    xp = x + 1 - 2 * lax.rem(x, 2)
    xpar = lax.rem(x, 2)

    def dev(xx, zz):
        return (y * NX + xx, zz * 2 + c)

    core = (leaf, z * 2 + other)

    def zp(d):
        return lax.rem(z + d, NZ)

    def zm(d):
        return lax.rem(z + NZ - d, NZ)

    def xq(d):
        return lax.rem(x + d, NX)

    def xm(d):
        return lax.rem(x + NX - d, NX)

    def at(value):
        return pl.multiple_of(value, UNIT)

    def copy(src, dst, sem, device):
        return pltpu.make_async_remote_copy(
            src_ref=src, dst_ref=dst, send_sem=ssem.at[sem], recv_sem=rsem.at[sem], device_id=device, device_id_type=MESH
        )

    def chains(body):
        def step(ch, carry):
            body(ch)
            return carry

        lax.fori_loop(0, CHAINS, step, 0)

    def cols(ch):
        return pl.ds(pl.multiple_of(ch * WIDTH, WIDTH), WIDTH)

    def gather_z(name, src, dst, ch):
        return [copy(src.at[ch], dst.at[ch, i], SEM_AT[name] + ch * 3 + i, dev(x, zp(d))) for i, d in enumerate(Z_PEERS)]

    def gather_pair(name, src, dst, ch):
        return [
            copy(src.at[ch], dst.at[ch, i], SEM_AT[name] + ch * 7 + i, dev(xp if px else x, zp(d)))
            for i, (px, d) in enumerate(PAIR_PEERS)
        ]

    def gather_quad(name, src, dst, ch):
        return [
            copy(src.at[ch], dst.at[ch, i], SEM_AT[name] + ch * 15 + i, dev(xq(dx), zp(d)))
            for i, (dx, d) in enumerate(QUAD_PEERS)
        ]

    def reduce_z(name, src, dst, ch):
        return [
            copy(src.at[ch, zp(d)], dst.at[ch, i], SEM_AT[name] + ch * 3 + i, dev(x, zp(d))) for i, d in enumerate(Z_PEERS)
        ]

    def reduce_pair(name, src, dst, ch):
        out = []
        for i, (px, d) in enumerate(PAIR_PEERS):
            xx = xp if px else x
            out.append(copy(src.at[ch, lax.rem(xx, 2), zp(d)], dst.at[ch, i], SEM_AT[name] + ch * 7 + i, dev(xx, zp(d))))
        return out

    def reduce_quad(name, src, dst, ch):
        return [
            copy(src.at[ch, xq(dx), zp(d)], dst.at[ch, i], SEM_AT[name] + ch * 15 + i, dev(xq(dx), zp(d)))
            for i, (dx, d) in enumerate(QUAD_PEERS)
        ]

    def x_quad(name, src, dst, ch):
        return [copy(src.at[ch, xq(d)], dst.at[ch, i], SEM_AT[name] + ch * 3 + i, dev(xq(d), z)) for i, d in enumerate(Z_PEERS)]

    def x_pair(name, src, dst, ch):
        return [copy(src.at[ch, 1 - xpar], dst.at[ch, 0], SEM_AT[name] + ch, dev(xp, z))]

    def start(copies):
        for one in copies:
            one.start()

    def received(copies):
        for one in copies:
            one.wait_recv()

    def sent(copies):
        for one in copies:
            one.wait_send()

    mine, theirs = pl.ds(pl.multiple_of(c * ROW, ROW), ROW), pl.ds(pl.multiple_of(other * ROW, ROW), ROW)
    spans = ((d_hbm, dm, 0, LEAF), (e_hbm, em, 0, LEAF), (d_hbm, dm, LEAF, 2 * LEAF), (e_hbm, em, LEAF, 2 * LEAF), (d_hbm, dm, 3 * LEAF, 4 * LEAF))

    load_rhs = pltpu.make_async_copy(rhs_hbm, rhs_v, lsem.at[0])
    load_rhs.start()
    loads = [
        pltpu.make_async_copy(src.at[:, pl.ds(a, n)], dst.at[mine, pl.ds(a, n)], lsem.at[1 + i])
        for i, (src, dst, a, n) in enumerate(spans)
    ]
    for one in loads:
        one.start()
    barrier = pltpu.get_barrier_semaphore()
    pl.semaphore_signal(barrier, inc=1, device_id=core, device_id_type=MESH)
    for dx, d in QUAD_PEERS:
        pl.semaphore_signal(barrier, inc=1, device_id=dev(xq(dx), zp(d)), device_id_type=MESH)

    eye = lax.broadcasted_iota(jnp.int32, (ROW, ROW), 0) == lax.broadcasted_iota(jnp.int32, (ROW, ROW), 1)
    for level in range(2):
        owner = jnp.sum(jnp.where(eye, owner_ref[level].astype(F32), 0.0), axis=0, keepdims=True).astype(jnp.int32)
        row = row_ref[level : level + 1, :]
        if level == 0:
            target = owner * ROW + row
        else:
            target = xpar * LEAF + (owner // 8) * (2 * LEAF) + lax.rem(owner, 8) * ROW + row
        tg[0, 0, level : level + 1, mine] = target

    load_rhs.wait()
    for level in range(3):
        rt[level, :, mine] = rhs_v[level, :, mine].astype(F32).T.astype(BF16)
        swap[level] = rhs_v[level, :, theirs].astype(F32).T.astype(BF16)

    pl.semaphore_wait(barrier, 16)
    swaps = [copy(swap.at[level], rt.at[level, :, mine], SEM_AT["core"] + level, core) for level in range(3)]
    swaps.append(copy(tg.at[0, 0, :, mine], tg.at[0, 0, :, mine], SEM_AT["core"] + 3, core))
    swaps += [
        copy(src.at[:, pl.ds(a, n)], dst.at[mine, pl.ds(a, n)], SEM_AT["core"] + 4 + i, core)
        for i, (src, dst, a, n) in enumerate(spans)
    ]
    start(swaps)

    def gather_r0(ch):
        return [
            copy(rt.at[0, cols(ch)], a0r.at[ch, i], SEM_AT["a0"] + ch * 3 + i, dev(x, zp(d))) for i, d in enumerate(Z_PEERS)
        ]

    swaps[0].wait_recv()
    chains(lambda ch: start(gather_r0(ch)))
    t_z = [copy(tg.at[0, 0], tg.at[0, d], SEM_AT["tz"] + i, dev(x, zp(d))) for i, d in enumerate(Z_PEERS)]
    t_x = [copy(tg.at[0], tg.at[d], SEM_AT["tx"] + i, dev(xq(d), z)) for i, d in enumerate(Z_PEERS)]
    r1_z = [copy(rt.at[1], zr1.at[0, d], SEM_AT["r1z"] + i, dev(x, zp(d))) for i, d in enumerate(Z_PEERS)]
    r2_z = [copy(rt.at[2], zr2.at[0, d], SEM_AT["r2z"] + i, dev(x, zp(d))) for i, d in enumerate(Z_PEERS)]
    r1_x = [copy(zr1.at[0], zr1.at[1], SEM_AT["r1x"], dev(xp, z))]
    r2_x = [copy(zr2.at[0], zr2.at[d], SEM_AT["r2x"] + i, dev(xq(d), z)) for i, d in enumerate(Z_PEERS)]
    swaps[3].wait_recv()
    start(t_z)
    swaps[1].wait_recv()
    start(r1_z)
    swaps[2].wait_recv()
    start(r2_z)
    zr1[0, 0] = rt[1]
    zr2[0, 0] = rt[2]

    def d_block(level, index):
        return dm[:, pl.ds(at(D_AT[level] + index * UNIT), UNIT)]

    def e_block(level, index):
        return em[:, pl.ds(at(E_AT[level] + index * UNIT), UNIT)]

    def pair_index(px, d):
        return lax.rem(xp if px else x, 2) * NZ + zm(d)

    loads[0].wait()
    swaps[4].wait_recv()

    def solve0(ch):
        total = nt(rt[0, cols(ch), :], d_block(0, z))
        for i, d in enumerate(Z_PEERS):
            gather_r0(ch)[i].wait_recv()
            total += nt(a0r[ch, i], d_block(0, zm(d)))
        s0b[ch] = total.astype(BF16)
        start(gather_z("a1", s0b, a1r, ch))

    chains(solve0)

    received(t_z)
    start(t_x)
    received(r1_z)
    start(r1_x)
    received(r2_z)
    start(r2_x)

    loads[1].wait()
    swaps[5].wait_recv()

    def update0(ch):
        total = nt(s0b[ch], e_block(0, z))
        copies = gather_z("a1", s0b, a1r, ch)
        for i, d in enumerate(Z_PEERS):
            copies[i].wait_recv()
            total += nt(a1r[ch, i], e_block(0, zm(d)))
        u0b[ch] = total.astype(BF16)
        start(gather_pair("u0", u0b, u0r, ch))

    chains(update0)

    def fill_select(target, base, count):
        for k in range(count):
            rows = lax.broadcasted_iota(jnp.int32, (UNIT, UNIT), 0) + (base + k * UNIT)
            select[k * UNIT : (k + 1) * UNIT, :] = jnp.where(rows == target, 1.0, 0.0).astype(BF16)

    loads[2].wait()
    swaps[6].wait_recv()
    received(t_x)

    def select1(j, carry):
        px, d = j // NZ, lax.rem(j, NZ)
        dx = px * (3 - 2 * xpar)
        source = lax.rem(x + px, 2) * NZ + zm(d)
        target = tg[dx, d, 0:1, :]
        total = jnp.zeros((UNIT, UNIT), F32)
        for part in range(2):
            fill_select(target, part * LEAF, 4)
            total += nn(dm[:, D_AT[1] + part * LEAF : D_AT[1] + (part + 1) * LEAF], select[...])
        m1[:, pl.ds(at(source * UNIT), UNIT)] = total.astype(BF16)
        return carry

    lax.fori_loop(0, 2 * NZ, select1, 0)
    received(r1_x)

    def rhs1(ch):
        total = jnp.zeros((WIDTH, UNIT), F32)
        for px in range(2):
            for d in range(NZ):
                total += nt(zr1[px, d, cols(ch), :], d_block(1, pair_index(px, d)))
        y1[ch] = total

    chains(rhs1)

    def solve1(ch):
        total = nt(u0b[ch], m1[:, pl.ds(at((xpar * NZ + z) * UNIT), UNIT)])
        copies = gather_pair("u0", u0b, u0r, ch)
        for i, (px, d) in reversed(list(enumerate(PAIR_PEERS))):
            copies[i].wait_recv()
            total += nt(u0r[ch, i], m1[:, pl.ds(at(pair_index(px, d) * UNIT), UNIT)])
        s1b[ch] = (y1[ch] - total).astype(BF16)
        start(gather_pair("s1", s1b, s1r, ch))

    chains(solve1)

    loads[4].wait()
    swaps[8].wait_recv()

    def select2(j, carry):
        dx, d = j // NZ, lax.rem(j, NZ)
        xj = xm(dx)
        target = tg[dx, d, 1:2, :]
        total = jnp.zeros((UNIT, UNIT), F32)
        for side in range(2):
            base = lax.rem(xj, 2) * LEAF + side * 2 * LEAF
            fill_select(target, base, 4)
            total += nn(dm[:, pl.ds(at(D_AT[2] + base), LEAF)], select[...])
        m2[:, pl.ds(at((xj * NZ + zm(d)) * UNIT), UNIT)] = total.astype(BF16)
        return carry

    lax.fori_loop(0, 8, select2, 0)

    loads[3].wait()
    swaps[7].wait_recv()

    def update1(ch):
        total = nt(s1b[ch], e_block(1, xpar * NZ + z))
        copies = gather_pair("s1", s1b, s1r, ch)
        for i, (px, d) in reversed(list(enumerate(PAIR_PEERS))):
            copies[i].wait_recv()
            total += nt(s1r[ch, i], e_block(1, pair_index(px, d)))
        u1b[ch] = total.astype(BF16)
        start(gather_quad("u1", u1b, u1r, ch))

    chains(update1)

    lax.fori_loop(8, 16, select2, 0)
    received(r2_x)

    def rhs2(ch):
        total = jnp.zeros((WIDTH, UNIT), F32)
        for dx in range(NX):
            for d in range(NZ):
                total += nt(zr2[dx, d, cols(ch), :], d_block(2, xm(dx) * NZ + zm(d)))
        y2[ch] = total

    chains(rhs2)

    def spread(matrix, base, vector, dst, ch, leaves):
        for k in range(leaves):
            part = nn(vector, matrix[:, base + k * LEAF : base + (k + 1) * LEAF]).astype(BF16)
            for i in range(NZ):
                if leaves == 1:
                    dst[ch, i] = part[:, i * UNIT : (i + 1) * UNIT]
                else:
                    dst[ch, k, i] = part[:, i * UNIT : (i + 1) * UNIT]

    def solve2(ch):
        total = nt(u1b[ch], m2[:, pl.ds(at((x * NZ + z) * UNIT), UNIT)])
        copies = gather_quad("u1", u1b, u1r, ch)
        for i, (dx, d) in reversed(list(enumerate(QUAD_PEERS))):
            copies[i].wait_recv()
            total += nt(u1r[ch, i], m2[:, pl.ds(at((xm(dx) * NZ + zm(d)) * UNIT), UNIT)])
        solved = (y2[ch] - total).astype(BF16)
        s2b[ch] = solved
        spread(m2, 0, solved, f1s, ch, 4)
        start(reduce_quad("f1", f1s, f1r, ch))

    chains(solve2)

    def back2(ch):
        spread(dm, D_AT[2], s2b[ch], d2xs, ch, 4)
        start(x_quad("d2x", d2xs, d2xr, ch))

    chains(back2)

    def summed(copies, own, dst, ch):
        total = own.astype(F32)
        for i in reversed(range(len(copies))):
            copies[i].wait_recv()
            total += dst[ch, i].astype(F32)
        return total

    def fetch1(ch):
        fetched = summed(reduce_quad("f1", f1s, f1r, ch), f1s[ch, x, z], f1r, ch).astype(BF16)
        spread(em, E_AT[1], fetched, e1s, ch, 2)
        start(reduce_pair("e1", e1s, e1r, ch))

    chains(fetch1)

    def weigh1(ch):
        carried = summed(reduce_pair("e1", e1s, e1r, ch), e1s[ch, xpar, z], e1r, ch)
        weights = (s1b[ch].astype(F32) - carried).astype(BF16)
        w1b[ch] = weights
        spread(m1, 0, weights, f0s, ch, 2)
        start(reduce_pair("f0", f0s, f0r, ch))

    chains(weigh1)

    def back2z(ch):
        received(x_quad("d2x", d2xs, d2xr, ch))
        for k in range(NZ):
            total = d2xs[ch, x, k].astype(F32)
            for i in range(3):
                total += d2xr[ch, i, k].astype(F32)
            d2zs[ch, k] = total.astype(BF16)
        start(reduce_z("d2z", d2zs, d2zr, ch))

    chains(back2z)

    def back1(ch):
        spread(dm, D_AT[1], w1b[ch], d1xs, ch, 2)
        start(x_pair("d1x", d1xs, d1xr, ch))

    chains(back1)

    def fetch0(ch):
        fetched = summed(reduce_pair("f0", f0s, f0r, ch), f0s[ch, xpar, z], f0r, ch).astype(BF16)
        spread(em, E_AT[0], fetched, w0s, ch, 1)
        start(reduce_z("w0", w0s, w0r, ch))

    chains(fetch0)

    def back1z(ch):
        received(x_pair("d1x", d1xs, d1xr, ch))
        for k in range(NZ):
            d1zs[ch, k] = (d1xs[ch, xpar, k].astype(F32) + d1xr[ch, 0, k].astype(F32)).astype(BF16)
        start(reduce_z("d1z", d1zs, d1zr, ch))

    chains(back1z)

    def weigh0(ch):
        carried = summed(reduce_z("w0", w0s, w0r, ch), w0s[ch, z], w0r, ch)
        weights = (s0b[ch].astype(F32) - carried).astype(BF16)
        spread(dm, D_AT[0], weights, l0s, ch, 1)
        start(reduce_z("l0", l0s, l0r, ch))

    chains(weigh0)

    def out_copies(level):
        keep = pltpu.make_async_copy(stage_own.at[level], out_hbm.at[level, :, mine], lsem.at[6 + level])
        hand = copy(stage_other.at[level], out_hbm.at[level, :, mine], SEM_AT["out"] + level, core)
        return keep, hand

    def finish(level, name, src, dst):
        def one(ch):
            sol[level, cols(ch), :] = summed(reduce_z(name, src, dst, ch), src[ch, z], dst, ch)

        chains(one)
        stage_other[level] = sol[level, :, theirs].T
        keep, hand = out_copies(level)
        hand.start()
        stage_own[level] = sol[level, :, mine].T
        keep.start()

    finish(2, "d2z", d2zs, d2zr)
    finish(1, "d1z", d1zs, d1zr)

    sent(swaps + t_z + t_x + r1_z + r1_x + r2_z + r2_x)

    def all_sent(ch):
        sent(gather_r0(ch))
        sent(gather_z("a1", s0b, a1r, ch))
        sent(gather_pair("u0", u0b, u0r, ch))
        sent(gather_pair("s1", s1b, s1r, ch))
        sent(gather_quad("u1", u1b, u1r, ch))
        sent(reduce_quad("f1", f1s, f1r, ch))
        sent(x_quad("d2x", d2xs, d2xr, ch))
        sent(reduce_z("d2z", d2zs, d2zr, ch))
        sent(reduce_pair("e1", e1s, e1r, ch))
        sent(reduce_pair("f0", f0s, f0r, ch))
        sent(x_pair("d1x", d1xs, d1xr, ch))
        sent(reduce_z("d1z", d1zs, d1zr, ch))
        sent(reduce_z("w0", w0s, w0r, ch))

    chains(all_sent)

    finish(0, "l0", l0s, l0r)
    chains(lambda ch: sent(reduce_z("l0", l0s, l0r, ch)))
    for level in range(3):
        keep, hand = out_copies(level)
        keep.wait()
        hand.wait()


def shards(rhs, inverse_blocks, update_blocks, asm_owner, asm_row):
    k, w = CHAINS, WIDTH
    vmem = pl.BlockSpec(memory_space=pltpu.VMEM)
    hbm = pl.BlockSpec(memory_space=pl.ANY)
    block = lambda *lead: pltpu.VMEM((k, *lead, w, UNIT), BF16)
    return pl.pallas_call(
        kernel,
        out_shape=jax.ShapeDtypeStruct(rhs.shape, F32),
        in_specs=[vmem, vmem, hbm, hbm, hbm],
        out_specs=hbm,
        scratch_shapes=[
            pltpu.VMEM((3, ROW, 2 * HALF), BF16),
            pltpu.VMEM((UNIT, 7 * LEAF), BF16),
            pltpu.VMEM((UNIT, 3 * LEAF), BF16),
            pltpu.VMEM((UNIT, 2 * LEAF), BF16),
            pltpu.VMEM((UNIT, 4 * LEAF), BF16),
            pltpu.VMEM((3, HALF, ROW), BF16),
            pltpu.VMEM((3, HALF, UNIT), BF16),
            pltpu.VMEM((NX, NZ, 8, UNIT), jnp.int32),
            pltpu.VMEM((2, NZ, HALF, UNIT), BF16),
            pltpu.VMEM((NX, NZ, HALF, UNIT), BF16),
            pltpu.VMEM((LEAF, UNIT), BF16),
            block(), block(), block(), block(), block(), block(),
            block(3), block(3), block(7), block(7), block(15),
            pltpu.VMEM((k, w, UNIT), F32),
            pltpu.VMEM((k, w, UNIT), F32),
            block(4, 4), block(15), block(2, 4), block(7), block(2, 4), block(7),
            block(4), block(3), block(4), block(3),
            block(4, 4), block(3, 4), block(4), block(3),
            block(2, 4), block(1, 4), block(4), block(3),
            pltpu.VMEM((3, HALF, UNIT), F32),
            pltpu.VMEM((3, ROW, HALF), F32),
            pltpu.VMEM((3, ROW, HALF), F32),
            pltpu.SemaphoreType.DMA((SEM_COUNT,)),
            pltpu.SemaphoreType.DMA((SEM_COUNT,)),
            pltpu.SemaphoreType.DMA((9,)),
        ],
        compiler_params=pltpu.CompilerParams(collective_id=0, has_side_effects=True, vmem_limit_bytes=56 * 2**20),
    )(asm_owner, asm_row, rhs, inverse_blocks, update_blocks)


def solution(mesh):
    placed = (
        P(None, ("leaf", "front"), None),
        P(("leaf", "front"), None),
        P(("leaf", "front"), None),
        P(None, ("leaf", "front"), None),
        P(None, ("leaf", "front")),
    )
    return jax.shard_map(
        shards, mesh=mesh, in_specs=placed, out_specs=P(None, ("leaf", "front"), None), check_vma=False
    )
```

time: 552 us -> 115 us (0.21)
  waiting for transfers between devices: 369 us -> 0 us
  Pallas kernels: 0 us -> 112 us
  blocking collectives: 109 us -> 0 us
  starting transfers between devices: 21 us -> 0 us
  matrix products: 20.6 us -> 0 us
  other arithmetic: 14.1 us -> 0 us
  between operations: 13.6 us -> 0.01 us
    reduce_scatter x7 -> x0, waiting for transfers between devices: 211 us -> none  [node_reduce(): lax.psum_scatter(partial_value.astype(jnp.bfloat16), 'front', scatter_dim...]
    ppermute x12 -> x0, waiting for transfers between devices: 158 us -> none  [swapped(): lax.ppermute(shard, axis, [(i, i ^ 1 << distance) for i in range(lax.axis...]
    pallas_call x0 -> x1, Pallas kernels: none -> 112 us  [shards(): pl.pallas_call(kernel, out_shape=jax.ShapeDtypeStruct(rhs.shape, F32), in...]
    all_gather x7 -> x0, blocking collectives: 109 us -> none  [node_gather(): gathered = lax.all_gather(local, 'front', axis=0, tiled=True)]
    ppermute x12 -> x0, starting transfers between devices: 20.8 us -> none  [swapped(): lax.ppermute(shard, axis, [(i, i ^ 1 << distance) for i in range(lax.axis...]
    dot_general x9 -> x0, matrix products: 20.6 us -> none  [the longest x7 18 us: contract_rows(): lax.dot_general(left, right, (((0,), (0,)), ((), ())), preferred_element_...]
    convert_element_type x13 -> x0, other arithmetic: 9.63 us -> none  [the longest x5 5.03 us: node_reduce(): partial_value.astype(jnp.bfloat16)]
  transfers between devices with their start and end apart: 19 -> 0, of which waited for: 19 -> 0; matrix products, arithmetic and copies ran while one was open for 0% -> 0% of each run, Pallas kernels for 0% -> 0%
where the time goes in v1:
time: 115 us
  Pallas kernels  112 us (97%)
  local copies, waits for them, and re-layouts  3.24 us (3%)
    pallas_call x1, Pallas kernels, shards(): pl.pallas_call(kernel, out_shape=jax.ShapeDtypeStruct(rhs.shape, F32), in...  112 us
    unnamed x2, local copies, waits for them, and re-layouts  3.24 us

profile of v1, /device:TPU:1, one launch (start us, length us, event | category | flops | bytes accessed | tf_op | source)
XLA Modules:
  0.0 115.2 jit_solution(415671159074043633)
XLA Ops:
  0.0 1.5 %copy.6.owner_ref = s32[2,128,1]{2,1,0:T(8,128)} copy(s32[2,128,1]{1,2,0:T(1,128)} %param.8) | data formatting | bytes 2048 | tf_op args[3]
  1.5 111.9 %shard_map.55 = f32[3,128,256]{2,1,0:T(8,128)} custom-call(s32[2,128,1]{2,1,0:T(8,128)} %copy.6.owner_ref, s32[2,128]{1,0:T(2,128)} %row_ref.1, bf16[3,128,256]{2,1,0:T(8,128)(2,1)} %rhs_hbm.1, bf16[128,7168]{1,0:T(8,128)(2,1)} %d_hbm.1, bf16[128,3072]{1,0:T(8,128)(2,1)} %e_hbm.1), custom_call_target="tpu_custom_call" | custom-call | tf_op jit(solution)/shard_map/pallas_call | solution.py:486
  113.4 1.8 %copy.8 = f32[3,128,256]{2,1,0:T(8,128)} copy(f32[3,128,256]{2,1,0:T(8,128)} %shard_map.55) | data formatting | bytes 786432

commit v2 on v1

--- a/solution.py
+++ b/solution.py
@@ -17,18 +17,19 @@
 NX, NZ = 4, 4
 LEAF = UNIT * NZ
 WIDTH = HALF // CHAINS
-D_AT = (0, LEAF, 3 * LEAF)
+D_AT = (0, LEAF)
 E_AT = (0, LEAF)
 
 Z_PEERS = (2, 1, 3)
 PAIR_PEERS = ((1, 2), (1, 1), (1, 3), (0, 2), (1, 0), (0, 1), (0, 3))
+X_PEERS = (2, 1, 3)
 QUAD_PEERS = tuple((dx, dz) for dx in (2, 1, 3, 0) for dz in (2, 1, 3, 0) if dx or dz)
 
 CHAINED = (
-    ("a0", 3), ("a1", 3), ("u0", 7), ("s1", 7), ("u1", 15), ("f1", 15), ("e1", 7), ("f0", 7), ("w0", 3), ("l0", 3),
-    ("d2x", 3), ("d2z", 3), ("d1x", 1), ("d1z", 3),
+    ("a0", 3), ("a1", 3), ("u0", 7), ("s1", 7), ("u1", 7), ("s2r", 3), ("s2a", 3), ("f1", 7), ("e1", 7), ("f0", 7),
+    ("w0", 3), ("l0", 3), ("d2z", 3), ("d1x", 1), ("d1z", 3),
 )
-SINGLE = (("core", 9), ("tz", 3), ("tx", 3), ("r1z", 3), ("r1x", 1), ("r2z", 3), ("r2x", 3), ("out", 3))
+SINGLE = (("core", 9), ("block", 3), ("hand", 3), ("tz", 3), ("tx", 3), ("r1z", 3), ("r1x", 1), ("r2z", 3), ("out", 3))
 SEM_AT, SEM_COUNT = {}, 0
 for _name, _n in CHAINED:
     SEM_AT[_name] = SEM_COUNT
@@ -48,11 +49,11 @@
 
 def kernel(
     owner_ref, row_ref, rhs_hbm, d_hbm, e_hbm, out_hbm,
-    rhs_v, dm, em, m1, m2, swap, rt, tg, zr1, zr2, select,
+    rhs_v, dm, d2, em, m1, m2, swap, rt, tg, zr1, zr2, select,
     s0b, u0b, s1b, u1b, s2b, w1b,
-    a0r, a1r, u0r, s1r, u1r, y1, y2,
+    a0r, a1r, u0r, s1r, u1r, y1, y2, s2rs, s2rr, s2ar,
     f1s, f1r, e1s, e1r, f0s, f0r, w0s, w0r, l0s, l0r,
-    d2xs, d2xr, d2zs, d2zr, d1xs, d1xr, d1zs, d1zr,
+    d2zs, d2zr, d1xs, d1xr, d1zs, d1zr,
     sol, stage_own, stage_other,
     ssem, rsem, lsem,
 ):
@@ -62,6 +63,7 @@
     other = 1 - c
     xp = x + 1 - 2 * lax.rem(x, 2)
     xpar = lax.rem(x, 2)
+    xo = lax.rem(x + 2, NX)
 
     def dev(xx, zz):
         return (y * NX + xx, zz * 2 + c)
@@ -107,11 +109,14 @@
             for i, (px, d) in enumerate(PAIR_PEERS)
         ]
 
-    def gather_quad(name, src, dst, ch):
+    def gather_skip(name, src, dst, ch):
         return [
-            copy(src.at[ch], dst.at[ch, i], SEM_AT[name] + ch * 15 + i, dev(xq(dx), zp(d)))
-            for i, (dx, d) in enumerate(QUAD_PEERS)
+            copy(src.at[ch], dst.at[ch, i], SEM_AT[name] + ch * 7 + i, dev(xo if px else x, zp(d)))
+            for i, (px, d) in enumerate(PAIR_PEERS)
         ]
+
+    def gather_x(name, src, dst, ch):
+        return [copy(src.at[ch], dst.at[ch, i], SEM_AT[name] + ch * 3 + i, dev(xq(d), z)) for i, d in enumerate(X_PEERS)]
 
     def reduce_z(name, src, dst, ch):
         return [
@@ -125,14 +130,15 @@
             out.append(copy(src.at[ch, lax.rem(xx, 2), zp(d)], dst.at[ch, i], SEM_AT[name] + ch * 7 + i, dev(xx, zp(d))))
         return out
 
-    def reduce_quad(name, src, dst, ch):
-        return [
-            copy(src.at[ch, xq(dx), zp(d)], dst.at[ch, i], SEM_AT[name] + ch * 15 + i, dev(xq(dx), zp(d)))
-            for i, (dx, d) in enumerate(QUAD_PEERS)
-        ]
-
-    def x_quad(name, src, dst, ch):
-        return [copy(src.at[ch, xq(d)], dst.at[ch, i], SEM_AT[name] + ch * 3 + i, dev(xq(d), z)) for i, d in enumerate(Z_PEERS)]
+    def reduce_skip(name, src, dst, ch):
+        out = []
+        for i, (px, d) in enumerate(PAIR_PEERS):
+            xx = xo if px else x
+            out.append(copy(src.at[ch, xx // 2, zp(d)], dst.at[ch, i], SEM_AT[name] + ch * 7 + i, dev(xx, zp(d))))
+        return out
+
+    def reduce_x(name, src, dst, ch):
+        return [copy(src.at[ch, xq(d)], dst.at[ch, i], SEM_AT[name] + ch * 3 + i, dev(xq(d), z)) for i, d in enumerate(X_PEERS)]
 
     def x_pair(name, src, dst, ch):
         return [copy(src.at[ch, 1 - xpar], dst.at[ch, 0], SEM_AT[name] + ch, dev(xp, z))]
@@ -150,7 +156,13 @@
             one.wait_send()
 
     mine, theirs = pl.ds(pl.multiple_of(c * ROW, ROW), ROW), pl.ds(pl.multiple_of(other * ROW, ROW), ROW)
-    spans = ((d_hbm, dm, 0, LEAF), (e_hbm, em, 0, LEAF), (d_hbm, dm, LEAF, 2 * LEAF), (e_hbm, em, LEAF, 2 * LEAF), (d_hbm, dm, 3 * LEAF, 4 * LEAF))
+    spans = ((d_hbm, dm, 0, LEAF), (e_hbm, em, 0, LEAF), (d_hbm, dm, LEAF, 2 * LEAF), (e_hbm, em, LEAF, 2 * LEAF))
+
+    def d2_columns(leaf_x):
+        return d_hbm.at[:, pl.ds(pl.multiple_of((3 + leaf_x) * LEAF, LEAF), LEAF)]
+
+    def d2_rows(leaf_x):
+        return d2.at[pl.ds(pl.multiple_of(leaf_x * UNIT + c * ROW, ROW), ROW)]
 
     load_rhs = pltpu.make_async_copy(rhs_hbm, rhs_v, lsem.at[0])
     load_rhs.start()
@@ -158,6 +170,7 @@
         pltpu.make_async_copy(src.at[:, pl.ds(a, n)], dst.at[mine, pl.ds(a, n)], lsem.at[1 + i])
         for i, (src, dst, a, n) in enumerate(spans)
     ]
+    loads.append(pltpu.make_async_copy(d2_columns(x), d2_rows(x), lsem.at[5]))
     for one in loads:
         one.start()
     barrier = pltpu.get_barrier_semaphore()
@@ -165,9 +178,8 @@
     for dx, d in QUAD_PEERS:
         pl.semaphore_signal(barrier, inc=1, device_id=dev(xq(dx), zp(d)), device_id_type=MESH)
 
-    eye = lax.broadcasted_iota(jnp.int32, (ROW, ROW), 0) == lax.broadcasted_iota(jnp.int32, (ROW, ROW), 1)
     for level in range(2):
-        owner = jnp.sum(jnp.where(eye, owner_ref[level].astype(F32), 0.0), axis=0, keepdims=True).astype(jnp.int32)
+        owner = owner_ref[level]
         row = row_ref[level : level + 1, :]
         if level == 0:
             target = owner * ROW + row
@@ -187,6 +199,7 @@
         copy(src.at[:, pl.ds(a, n)], dst.at[mine, pl.ds(a, n)], SEM_AT["core"] + 4 + i, core)
         for i, (src, dst, a, n) in enumerate(spans)
     ]
+    swaps.append(copy(d2_columns(x), d2_rows(x), SEM_AT["core"] + 8, core))
     start(swaps)
 
     def gather_r0(ch):
@@ -198,18 +211,17 @@
     chains(lambda ch: start(gather_r0(ch)))
     t_z = [copy(tg.at[0, 0], tg.at[0, d], SEM_AT["tz"] + i, dev(x, zp(d))) for i, d in enumerate(Z_PEERS)]
     t_x = [copy(tg.at[0], tg.at[d], SEM_AT["tx"] + i, dev(xq(d), z)) for i, d in enumerate(Z_PEERS)]
-    r1_z = [copy(rt.at[1], zr1.at[0, d], SEM_AT["r1z"] + i, dev(x, zp(d))) for i, d in enumerate(Z_PEERS)]
-    r2_z = [copy(rt.at[2], zr2.at[0, d], SEM_AT["r2z"] + i, dev(x, zp(d))) for i, d in enumerate(Z_PEERS)]
-    r1_x = [copy(zr1.at[0], zr1.at[1], SEM_AT["r1x"], dev(xp, z))]
-    r2_x = [copy(zr2.at[0], zr2.at[d], SEM_AT["r2x"] + i, dev(xq(d), z)) for i, d in enumerate(Z_PEERS)]
+    r1_x = [copy(rt.at[1], zr1.at[1, 0], SEM_AT["r1x"], dev(xp, z))]
+    r1_z = [copy(zr1.at[:, 0], zr1.at[:, d], SEM_AT["r1z"] + i, dev(x, zp(d))) for i, d in enumerate(Z_PEERS)]
+    r2_z = [copy(rt.at[2], zr2.at[d], SEM_AT["r2z"] + i, dev(x, zp(d))) for i, d in enumerate(Z_PEERS)]
+    blocks = [copy(d2_columns(xq(d)), d2_rows(x), SEM_AT["block"] + i, dev(xq(d), z)) for i, d in enumerate(X_PEERS)]
+    hands = [copy(d2_rows(xm(d)), d2_rows(xm(d)), SEM_AT["hand"] + i, core) for i, d in enumerate(X_PEERS)]
     swaps[3].wait_recv()
     start(t_z)
     swaps[1].wait_recv()
-    start(r1_z)
-    swaps[2].wait_recv()
-    start(r2_z)
+    start(r1_x)
+    start(blocks)
     zr1[0, 0] = rt[1]
-    zr2[0, 0] = rt[2]
 
     def d_block(level, index):
         return dm[:, pl.ds(at(D_AT[level] + index * UNIT), UNIT)]
@@ -235,10 +247,8 @@
 
     received(t_z)
     start(t_x)
-    received(r1_z)
-    start(r1_x)
-    received(r2_z)
-    start(r2_x)
+    received(r1_x)
+    start(r1_z)
 
     loads[1].wait()
     swaps[5].wait_recv()
@@ -276,7 +286,7 @@
         return carry
 
     lax.fori_loop(0, 2 * NZ, select1, 0)
-    received(r1_x)
+    received(r1_z)
 
     def rhs1(ch):
         total = jnp.zeros((WIDTH, UNIT), F32)
@@ -298,22 +308,26 @@
 
     chains(solve1)
 
+    swaps[2].wait_recv()
+    start(r2_z)
+    for i in range(3):
+        blocks[i].wait_recv()
+        hands[i].start()
     loads[4].wait()
     swaps[8].wait_recv()
+    received(hands)
 
     def select2(j, carry):
-        dx, d = j // NZ, lax.rem(j, NZ)
-        xj = xm(dx)
-        target = tg[dx, d, 1:2, :]
-        total = jnp.zeros((UNIT, UNIT), F32)
-        for side in range(2):
-            base = lax.rem(xj, 2) * LEAF + side * 2 * LEAF
-            fill_select(target, base, 4)
-            total += nn(dm[:, pl.ds(at(D_AT[2] + base), LEAF)], select[...])
-        m2[:, pl.ds(at((xj * NZ + zm(d)) * UNIT), UNIT)] = total.astype(BF16)
+        side, zz = j // NZ, lax.rem(j, NZ)
+        dx = lax.rem(x // 2 + side, 2) * 2
+        target = tg[dx, lax.rem(z + NZ - zz, NZ), 1:2, :]
+        fill_select(target, x * LEAF, 4)
+        for k in range(NX):
+            chosen = nn(d2[k * UNIT : (k + 1) * UNIT, :], select[...])
+            m2[k * UNIT : (k + 1) * UNIT, pl.ds(at(j * UNIT), UNIT)] = chosen.astype(BF16)
         return carry
 
-    lax.fori_loop(0, 8, select2, 0)
+    lax.fori_loop(0, 4, select2, 0)
 
     loads[3].wait()
     swaps[7].wait_recv()
@@ -325,18 +339,17 @@
             copies[i].wait_recv()
             total += nt(s1r[ch, i], e_block(1, pair_index(px, d)))
         u1b[ch] = total.astype(BF16)
-        start(gather_quad("u1", u1b, u1r, ch))
+        start(gather_skip("u1", u1b, u1r, ch))
 
     chains(update1)
 
-    lax.fori_loop(8, 16, select2, 0)
-    received(r2_x)
+    lax.fori_loop(4, 8, select2, 0)
+    received(r2_z)
 
     def rhs2(ch):
-        total = jnp.zeros((WIDTH, UNIT), F32)
-        for dx in range(NX):
-            for d in range(NZ):
-                total += nt(zr2[dx, d, cols(ch), :], d_block(2, xm(dx) * NZ + zm(d)))
+        total = nt(rt[2, cols(ch), :], d2[:, pl.ds(at(z * UNIT), UNIT)])
+        for d in range(1, NZ):
+            total += nt(zr2[d, cols(ch), :], d2[:, pl.ds(at(zm(d) * UNIT), UNIT)])
         y2[ch] = total
 
     chains(rhs2)
@@ -350,24 +363,21 @@
                 else:
                     dst[ch, k, i] = part[:, i * UNIT : (i + 1) * UNIT]
 
+    def skip_columns(px, d):
+        return m2[:, pl.ds(at(((xo if px else x) // 2 * NZ + zm(d)) * UNIT), UNIT)]
+
     def solve2(ch):
-        total = nt(u1b[ch], m2[:, pl.ds(at((x * NZ + z) * UNIT), UNIT)])
-        copies = gather_quad("u1", u1b, u1r, ch)
-        for i, (dx, d) in reversed(list(enumerate(QUAD_PEERS))):
+        total = y2[ch] - nt(u1b[ch], skip_columns(0, 0))
+        copies = gather_skip("u1", u1b, u1r, ch)
+        for i, (px, d) in reversed(list(enumerate(PAIR_PEERS))):
             copies[i].wait_recv()
-            total += nt(u1r[ch, i], m2[:, pl.ds(at((xm(dx) * NZ + zm(d)) * UNIT), UNIT)])
-        solved = (y2[ch] - total).astype(BF16)
-        s2b[ch] = solved
-        spread(m2, 0, solved, f1s, ch, 4)
-        start(reduce_quad("f1", f1s, f1r, ch))
+            total -= nt(u1r[ch, i], skip_columns(px, d))
+        part = total.astype(BF16)
+        for k in range(NX):
+            s2rs[ch, k] = part[:, k * UNIT : (k + 1) * UNIT]
+        start(reduce_x("s2r", s2rs, s2rr, ch))
 
     chains(solve2)
-
-    def back2(ch):
-        spread(dm, D_AT[2], s2b[ch], d2xs, ch, 4)
-        start(x_quad("d2x", d2xs, d2xr, ch))
-
-    chains(back2)
 
     def summed(copies, own, dst, ch):
         total = own.astype(F32)
@@ -376,8 +386,58 @@
             total += dst[ch, i].astype(F32)
         return total
 
+    def share2(ch):
+        s2b[ch] = summed(reduce_x("s2r", s2rs, s2rr, ch), s2rs[ch, x], s2rr, ch).astype(BF16)
+        start(gather_x("s2a", s2b, s2ar, ch))
+
+    chains(share2)
+
+    def row_block(matrix, index, first, count):
+        return matrix[pl.ds(at(index * UNIT), UNIT), first : first + count]
+
+    def fetch2(ch):
+        copies = gather_x("s2a", s2b, s2ar, ch)
+        received(copies)
+        for side in range(2):
+            total = nn(s2b[ch], row_block(m2, x, side * LEAF, LEAF))
+            for i, d in enumerate(X_PEERS):
+                total += nn(s2ar[ch, i], row_block(m2, xm(d), side * LEAF, LEAF))
+            part = total.astype(BF16)
+            for i in range(NZ):
+                f1s[ch, side, i] = part[:, i * UNIT : (i + 1) * UNIT]
+        start(reduce_skip("f1", f1s, f1r, ch))
+
+    chains(fetch2)
+
+    def back2(ch):
+        total = nn(s2b[ch], row_block(d2, x, 0, LEAF))
+        for i, d in enumerate(X_PEERS):
+            total += nn(s2ar[ch, i], row_block(d2, xm(d), 0, LEAF))
+        part = total.astype(BF16)
+        for i in range(NZ):
+            d2zs[ch, i] = part[:, i * UNIT : (i + 1) * UNIT]
+        start(reduce_z("d2z", d2zs, d2zr, ch))
+
+    chains(back2)
+
+    def out_copies(level):
+        keep = pltpu.make_async_copy(stage_own.at[level], out_hbm.at[level, :, mine], lsem.at[6 + level])
+        hand = copy(stage_other.at[level], out_hbm.at[level, :, mine], SEM_AT["out"] + level, core)
+        return keep, hand
+
+    def finish(level, name, src, dst):
+        def one(ch):
+            sol[level, cols(ch), :] = summed(reduce_z(name, src, dst, ch), src[ch, z], dst, ch)
+
+        chains(one)
+        stage_other[level] = sol[level, :, theirs].T
+        keep, hand = out_copies(level)
+        hand.start()
+        stage_own[level] = sol[level, :, mine].T
+        keep.start()
+
     def fetch1(ch):
-        fetched = summed(reduce_quad("f1", f1s, f1r, ch), f1s[ch, x, z], f1r, ch).astype(BF16)
+        fetched = summed(reduce_skip("f1", f1s, f1r, ch), f1s[ch, x // 2, z], f1r, ch).astype(BF16)
         spread(em, E_AT[1], fetched, e1s, ch, 2)
         start(reduce_pair("e1", e1s, e1r, ch))
 
@@ -392,22 +452,12 @@
 
     chains(weigh1)
 
-    def back2z(ch):
-        received(x_quad("d2x", d2xs, d2xr, ch))
-        for k in range(NZ):
-            total = d2xs[ch, x, k].astype(F32)
-            for i in range(3):
-                total += d2xr[ch, i, k].astype(F32)
-            d2zs[ch, k] = total.astype(BF16)
-        start(reduce_z("d2z", d2zs, d2zr, ch))
-
-    chains(back2z)
-
     def back1(ch):
         spread(dm, D_AT[1], w1b[ch], d1xs, ch, 2)
         start(x_pair("d1x", d1xs, d1xr, ch))
 
     chains(back1)
+    finish(2, "d2z", d2zs, d2zr)
 
     def fetch0(ch):
         fetched = summed(reduce_pair("f0", f0s, f0r, ch), f0s[ch, xpar, z], f0r, ch).astype(BF16)
@@ -431,36 +481,19 @@
         start(reduce_z("l0", l0s, l0r, ch))
 
     chains(weigh0)
-
-    def out_copies(level):
-        keep = pltpu.make_async_copy(stage_own.at[level], out_hbm.at[level, :, mine], lsem.at[6 + level])
-        hand = copy(stage_other.at[level], out_hbm.at[level, :, mine], SEM_AT["out"] + level, core)
-        return keep, hand
-
-    def finish(level, name, src, dst):
-        def one(ch):
-            sol[level, cols(ch), :] = summed(reduce_z(name, src, dst, ch), src[ch, z], dst, ch)
-
-        chains(one)
-        stage_other[level] = sol[level, :, theirs].T
-        keep, hand = out_copies(level)
-        hand.start()
-        stage_own[level] = sol[level, :, mine].T
-        keep.start()
-
-    finish(2, "d2z", d2zs, d2zr)
     finish(1, "d1z", d1zs, d1zr)
 
-    sent(swaps + t_z + t_x + r1_z + r1_x + r2_z + r2_x)
+    sent(swaps + blocks + hands + t_z + t_x + r1_x + r1_z + r2_z)
 
     def all_sent(ch):
         sent(gather_r0(ch))
         sent(gather_z("a1", s0b, a1r, ch))
         sent(gather_pair("u0", u0b, u0r, ch))
         sent(gather_pair("s1", s1b, s1r, ch))
-        sent(gather_quad("u1", u1b, u1r, ch))
-        sent(reduce_quad("f1", f1s, f1r, ch))
-        sent(x_quad("d2x", d2xs, d2xr, ch))
+        sent(gather_skip("u1", u1b, u1r, ch))
+        sent(reduce_x("s2r", s2rs, s2rr, ch))
+        sent(gather_x("s2a", s2b, s2ar, ch))
+        sent(reduce_skip("f1", f1s, f1r, ch))
         sent(reduce_z("d2z", d2zs, d2zr, ch))
         sent(reduce_pair("e1", e1s, e1r, ch))
         sent(reduce_pair("f0", f0s, f0r, ch))
@@ -490,23 +523,25 @@
         out_specs=hbm,
         scratch_shapes=[
             pltpu.VMEM((3, ROW, 2 * HALF), BF16),
-            pltpu.VMEM((UNIT, 7 * LEAF), BF16),
+            pltpu.VMEM((UNIT, 3 * LEAF), BF16),
+            pltpu.VMEM((LEAF, LEAF), BF16),
             pltpu.VMEM((UNIT, 3 * LEAF), BF16),
             pltpu.VMEM((UNIT, 2 * LEAF), BF16),
-            pltpu.VMEM((UNIT, 4 * LEAF), BF16),
+            pltpu.VMEM((LEAF, 2 * LEAF), BF16),
             pltpu.VMEM((3, HALF, ROW), BF16),
             pltpu.VMEM((3, HALF, UNIT), BF16),
             pltpu.VMEM((NX, NZ, 8, UNIT), jnp.int32),
             pltpu.VMEM((2, NZ, HALF, UNIT), BF16),
-            pltpu.VMEM((NX, NZ, HALF, UNIT), BF16),
+            pltpu.VMEM((NZ, HALF, UNIT), BF16),
             pltpu.VMEM((LEAF, UNIT), BF16),
             block(), block(), block(), block(), block(), block(),
-            block(3), block(3), block(7), block(7), block(15),
+            block(3), block(3), block(7), block(7), block(7),
             pltpu.VMEM((k, w, UNIT), F32),
-            pltpu.VMEM((k, w, UNIT), F32),
-            block(4, 4), block(15), block(2, 4), block(7), block(2, 4), block(7),
+            pltpu.VMEM((k, w, LEAF), F32),
+            block(4), block(3), block(3),
+            block(2, 4), block(7), block(2, 4), block(7), block(2, 4), block(7),
             block(4), block(3), block(4), block(3),
-            block(4, 4), block(3, 4), block(4), block(3),
+            block(4), block(3),
             block(2, 4), block(1, 4), block(4), block(3),
             pltpu.VMEM((3, HALF, UNIT), F32),
             pltpu.VMEM((3, ROW, HALF), F32),
@@ -516,7 +551,7 @@
             pltpu.SemaphoreType.DMA((9,)),
         ],
         compiler_params=pltpu.CompilerParams(collective_id=0, has_side_effects=True, vmem_limit_bytes=56 * 2**20),
-    )(asm_owner, asm_row, rhs, inverse_blocks, update_blocks)
+    )(asm_owner.reshape(asm_row.shape[0], 1, asm_row.shape[1]), asm_row, rhs, inverse_blocks, update_blocks)
 
 
 def solution(mesh):

time: 115 us -> 95.5 us (0.83)
  Pallas kernels: 112 us -> 93.6 us
  local copies, waits for them, and re-layouts: 3.24 us -> 1.77 us
    pallas_call x1, Pallas kernels: 112 us -> 93.6 us  [shards(): pl.pallas_call(kernel, out_shape=jax.ShapeDtypeStruct(rhs.shape, F32), in...]
    unnamed x2 -> x1, local copies, waits for them, and re-layouts: 3.24 us -> 1.77 us
where the time goes in v2:
time: 95.5 us; the launch traced here: 95.4 us
  Pallas kernels  93.6 us (98%)
  local copies, waits for them, and re-layouts  1.77 us (2%)
    pallas_call x1, Pallas kernels, shards(): pl.pallas_call(kernel, out_shape=jax.ShapeDtypeStruct(rhs.shape, F32), in...  93.6 us

profile of v2, /device:TPU:1, one launch (start us, length us, event | category | flops | bytes accessed | tf_op | source)
XLA Modules:
  0.0 95.4 jit_solution(13156821105256940027)
XLA Ops:
  0.0 93.6 %shard_map.55 = f32[3,128,256]{2,1,0:T(8,128)} custom-call(s32[2,1,128]{2,1,0:T(1,128)} %bitcast.1, s32[2,128]{1,0:T(2,128)} %row_ref.1, bf16[3,128,256]{2,1,0:T(8,128)(2,1)} %rhs_hbm.1, bf16[128,7168]{1,0:T(8,128)(2,1)} %d_hbm.1, bf16[128,3072]{1,0:T(8,128)(2,1)} %e_hbm.1), custom_call_target="tpu_custom_call" | custom-call | tf_op jit(solution)/shard_map/pallas_call | solution.py:519
  93.6 1.8 %copy.7 = f32[3,128,256]{2,1,0:T(8,128)} copy(f32[3,128,256]{2,1,0:T(8,128)} %shard_map.55) | data formatting | bytes 786432

commit v3 on v2

--- a/solution.py
+++ b/solution.py
@@ -26,10 +26,10 @@
 QUAD_PEERS = tuple((dx, dz) for dx in (2, 1, 3, 0) for dz in (2, 1, 3, 0) if dx or dz)
 
 CHAINED = (
-    ("a0", 3), ("a1", 3), ("u0", 7), ("s1", 7), ("u1", 7), ("s2r", 3), ("s2a", 3), ("f1", 7), ("e1", 7), ("f0", 7),
+    ("a1", 3), ("u0", 7), ("s1", 7), ("u1", 7), ("s2r", 3), ("s2a", 3), ("f1", 7), ("e1", 7), ("f0", 7),
     ("w0", 3), ("l0", 3), ("d2z", 3), ("d1x", 1), ("d1z", 3),
 )
-SINGLE = (("core", 9), ("block", 3), ("hand", 3), ("tz", 3), ("tx", 3), ("r1z", 3), ("r1x", 1), ("r2z", 3), ("out", 3))
+SINGLE = (("a0", 3), ("a0x", 3), ("core", 9), ("block", 3), ("hand", 3), ("tz", 3), ("tx", 3), ("r1z", 3), ("r1x", 1), ("r2z", 3), ("out", 3))
 SEM_AT, SEM_COUNT = {}, 0
 for _name, _n in CHAINED:
     SEM_AT[_name] = SEM_COUNT
@@ -48,10 +48,10 @@
 
 
 def kernel(
-    owner_ref, row_ref, rhs_hbm, d_hbm, e_hbm, out_hbm,
-    rhs_v, dm, d2, em, m1, m2, swap, rt, tg, zr1, zr2, select,
+    owner_hbm, row_hbm, rhs_hbm, d_hbm, e_hbm, out_hbm,
+    owner_ref, row_ref, rhs_v, dm, d2, em, m1, m2, swap, rt, tg, zr1, zr2, select,
     s0b, u0b, s1b, u1b, s2b, w1b,
-    a0r, a1r, u0r, s1r, u1r, y1, y2, s2rs, s2rr, s2ar,
+    a0, a1r, u0r, s1r, u1r, y1, y2, s2rs, s2rr, s2ar,
     f1s, f1r, e1s, e1r, f0s, f0r, w0s, w0r, l0s, l0r,
     d2zs, d2zr, d1xs, d1xr, d1zs, d1zr,
     sol, stage_own, stage_other,
@@ -70,6 +70,9 @@
 
     core = (leaf, z * 2 + other)
 
+    def dev_other(zz):
+        return (leaf, zz * 2 + other)
+
     def zp(d):
         return lax.rem(z + d, NZ)
 
@@ -164,8 +167,12 @@
     def d2_rows(leaf_x):
         return d2.at[pl.ds(pl.multiple_of(leaf_x * UNIT + c * ROW, ROW), ROW)]
 
-    load_rhs = pltpu.make_async_copy(rhs_hbm, rhs_v, lsem.at[0])
-    load_rhs.start()
+    load_rhs = [pltpu.make_async_copy(rhs_hbm.at[level], rhs_v.at[level], lsem.at[9 + level]) for level in range(3)]
+    load_lists = [
+        pltpu.make_async_copy(owner_hbm, owner_ref, lsem.at[12]), pltpu.make_async_copy(row_hbm, row_ref, lsem.at[0])
+    ]
+    for one in load_rhs + load_lists:
+        one.start()
     loads = [
         pltpu.make_async_copy(src.at[:, pl.ds(a, n)], dst.at[mine, pl.ds(a, n)], lsem.at[1 + i])
         for i, (src, dst, a, n) in enumerate(spans)
@@ -177,7 +184,38 @@
     pl.semaphore_signal(barrier, inc=1, device_id=core, device_id_type=MESH)
     for dx, d in QUAD_PEERS:
         pl.semaphore_signal(barrier, inc=1, device_id=dev(xq(dx), zp(d)), device_id_type=MESH)
-
+    for d in Z_PEERS:
+        pl.semaphore_signal(barrier, inc=1, device_id=dev_other(zp(d)), device_id_type=MESH)
+
+    def turn(level, own):
+        load_rhs[level].wait()
+        swap[level] = rhs_v[level, :, theirs].astype(F32).T.astype(BF16)
+        own[:, mine] = rhs_v[level, :, mine].astype(F32).T.astype(BF16)
+
+    turn(0, a0.at[0])
+    pl.semaphore_wait(barrier, 19)
+    half = a0.at[0, :, mine]
+    r0_same = [copy(half, a0.at[d, :, mine], SEM_AT["a0"] + i, dev(x, zp(d))) for i, d in enumerate(Z_PEERS)]
+    r0_cross = [copy(swap.at[0], a0.at[d, :, mine], SEM_AT["a0x"] + i, dev_other(zp(d))) for i, d in enumerate(Z_PEERS)]
+    for i in range(3):
+        r0_same[i].start()
+        r0_cross[i].start()
+    swaps = [copy(swap.at[0], half, SEM_AT["core"], core)]
+    swaps += [copy(swap.at[level], rt.at[level, :, mine], SEM_AT["core"] + level, core) for level in (1, 2)]
+    swaps.append(copy(tg.at[0, 0, :, mine], tg.at[0, 0, :, mine], SEM_AT["core"] + 3, core))
+    swaps += [
+        copy(src.at[:, pl.ds(a, n)], dst.at[mine, pl.ds(a, n)], SEM_AT["core"] + 4 + i, core)
+        for i, (src, dst, a, n) in enumerate(spans)
+    ]
+    swaps.append(copy(d2_columns(x), d2_rows(x), SEM_AT["core"] + 8, core))
+    swaps[0].start()
+    swaps[4].start()
+    turn(1, rt.at[1])
+    swaps[1].start()
+    swaps[5].start()
+
+    for one in load_lists:
+        one.wait()
     for level in range(2):
         owner = owner_ref[level]
         row = row_ref[level : level + 1, :]
@@ -186,29 +224,12 @@
         else:
             target = xpar * LEAF + (owner // 8) * (2 * LEAF) + lax.rem(owner, 8) * ROW + row
         tg[0, 0, level : level + 1, mine] = target
-
-    load_rhs.wait()
-    for level in range(3):
-        rt[level, :, mine] = rhs_v[level, :, mine].astype(F32).T.astype(BF16)
-        swap[level] = rhs_v[level, :, theirs].astype(F32).T.astype(BF16)
-
-    pl.semaphore_wait(barrier, 16)
-    swaps = [copy(swap.at[level], rt.at[level, :, mine], SEM_AT["core"] + level, core) for level in range(3)]
-    swaps.append(copy(tg.at[0, 0, :, mine], tg.at[0, 0, :, mine], SEM_AT["core"] + 3, core))
-    swaps += [
-        copy(src.at[:, pl.ds(a, n)], dst.at[mine, pl.ds(a, n)], SEM_AT["core"] + 4 + i, core)
-        for i, (src, dst, a, n) in enumerate(spans)
-    ]
-    swaps.append(copy(d2_columns(x), d2_rows(x), SEM_AT["core"] + 8, core))
-    start(swaps)
-
-    def gather_r0(ch):
-        return [
-            copy(rt.at[0, cols(ch)], a0r.at[ch, i], SEM_AT["a0"] + ch * 3 + i, dev(x, zp(d))) for i, d in enumerate(Z_PEERS)
-        ]
-
-    swaps[0].wait_recv()
-    chains(lambda ch: start(gather_r0(ch)))
+    swaps[3].start()
+    turn(2, rt.at[2])
+    swaps[2].start()
+    for i in (6, 7, 8):
+        swaps[i].start()
+
     t_z = [copy(tg.at[0, 0], tg.at[0, d], SEM_AT["tz"] + i, dev(x, zp(d))) for i, d in enumerate(Z_PEERS)]
     t_x = [copy(tg.at[0], tg.at[d], SEM_AT["tx"] + i, dev(xq(d), z)) for i, d in enumerate(Z_PEERS)]
     r1_x = [copy(rt.at[1], zr1.at[1, 0], SEM_AT["r1x"], dev(xp, z))]
@@ -236,13 +257,14 @@
     swaps[4].wait_recv()
 
     def solve0(ch):
-        total = nt(rt[0, cols(ch), :], d_block(0, z))
-        for i, d in enumerate(Z_PEERS):
-            gather_r0(ch)[i].wait_recv()
-            total += nt(a0r[ch, i], d_block(0, zm(d)))
+        total = nt(a0[0, cols(ch), :], d_block(0, z))
+        for d in range(1, NZ):
+            total += nt(a0[d, cols(ch), :], d_block(0, zm(d)))
         s0b[ch] = total.astype(BF16)
         start(gather_z("a1", s0b, a1r, ch))
 
+    swaps[0].wait_recv()
+    received(r0_same + r0_cross)
     chains(solve0)
 
     received(t_z)
@@ -250,28 +272,10 @@
     received(r1_x)
     start(r1_z)
 
-    loads[1].wait()
-    swaps[5].wait_recv()
-
-    def update0(ch):
-        total = nt(s0b[ch], e_block(0, z))
-        copies = gather_z("a1", s0b, a1r, ch)
-        for i, d in enumerate(Z_PEERS):
-            copies[i].wait_recv()
-            total += nt(a1r[ch, i], e_block(0, zm(d)))
-        u0b[ch] = total.astype(BF16)
-        start(gather_pair("u0", u0b, u0r, ch))
-
-    chains(update0)
-
     def fill_select(target, base, count):
         for k in range(count):
             rows = lax.broadcasted_iota(jnp.int32, (UNIT, UNIT), 0) + (base + k * UNIT)
             select[k * UNIT : (k + 1) * UNIT, :] = jnp.where(rows == target, 1.0, 0.0).astype(BF16)
-
-    loads[2].wait()
-    swaps[6].wait_recv()
-    received(t_x)
 
     def select1(j, carry):
         px, d = j // NZ, lax.rem(j, NZ)
@@ -285,7 +289,26 @@
         m1[:, pl.ds(at(source * UNIT), UNIT)] = total.astype(BF16)
         return carry
 
-    lax.fori_loop(0, 2 * NZ, select1, 0)
+    loads[2].wait()
+    swaps[6].wait_recv()
+    lax.fori_loop(0, 3, select1, 0)
+    loads[1].wait()
+    swaps[5].wait_recv()
+
+    def update0(ch):
+        total = nt(s0b[ch], e_block(0, z))
+        copies = gather_z("a1", s0b, a1r, ch)
+        for i, d in enumerate(Z_PEERS):
+            copies[i].wait_recv()
+            total += nt(a1r[ch, i], e_block(0, zm(d)))
+        u0b[ch] = total.astype(BF16)
+        start(gather_pair("u0", u0b, u0r, ch))
+
+    chains(update0)
+
+    received(t_x)
+
+    lax.fori_loop(3, 2 * NZ, select1, 0)
     received(r1_z)
 
     def rhs1(ch):
@@ -322,9 +345,7 @@
         dx = lax.rem(x // 2 + side, 2) * 2
         target = tg[dx, lax.rem(z + NZ - zz, NZ), 1:2, :]
         fill_select(target, x * LEAF, 4)
-        for k in range(NX):
-            chosen = nn(d2[k * UNIT : (k + 1) * UNIT, :], select[...])
-            m2[k * UNIT : (k + 1) * UNIT, pl.ds(at(j * UNIT), UNIT)] = chosen.astype(BF16)
+        m2[:, pl.ds(at(j * UNIT), UNIT)] = nn(d2[...], select[...]).astype(BF16)
         return carry
 
     lax.fori_loop(0, 4, select2, 0)
@@ -391,23 +412,35 @@
         start(gather_x("s2a", s2b, s2ar, ch))
 
     chains(share2)
+    sent(swaps + r0_same + r0_cross + blocks + hands + t_z + t_x + r1_x + r1_z + r2_z)
 
     def row_block(matrix, index, first, count):
         return matrix[pl.ds(at(index * UNIT), UNIT), first : first + count]
 
     def fetch2(ch):
         copies = gather_x("s2a", s2b, s2ar, ch)
-        received(copies)
+        totals = [nn(s2b[ch], row_block(m2, x, side * LEAF, LEAF)) for side in range(2)]
+        for i, d in reversed(list(enumerate(X_PEERS))):
+            copies[i].wait_recv()
+            for side in range(2):
+                totals[side] += nn(s2ar[ch, i], row_block(m2, xm(d), side * LEAF, LEAF))
         for side in range(2):
-            total = nn(s2b[ch], row_block(m2, x, side * LEAF, LEAF))
-            for i, d in enumerate(X_PEERS):
-                total += nn(s2ar[ch, i], row_block(m2, xm(d), side * LEAF, LEAF))
-            part = total.astype(BF16)
+            part = totals[side].astype(BF16)
             for i in range(NZ):
                 f1s[ch, side, i] = part[:, i * UNIT : (i + 1) * UNIT]
         start(reduce_skip("f1", f1s, f1r, ch))
 
     chains(fetch2)
+
+    def sent_forward(ch):
+        sent(gather_z("a1", s0b, a1r, ch))
+        sent(gather_pair("u0", u0b, u0r, ch))
+        sent(gather_pair("s1", s1b, s1r, ch))
+        sent(gather_skip("u1", u1b, u1r, ch))
+        sent(reduce_x("s2r", s2rs, s2rr, ch))
+        sent(gather_x("s2a", s2b, s2ar, ch))
+
+    chains(sent_forward)
 
     def back2(ch):
         total = nn(s2b[ch], row_block(d2, x, 0, LEAF))
@@ -418,8 +451,6 @@
             d2zs[ch, i] = part[:, i * UNIT : (i + 1) * UNIT]
         start(reduce_z("d2z", d2zs, d2zr, ch))
 
-    chains(back2)
-
     def out_copies(level):
         keep = pltpu.make_async_copy(stage_own.at[level], out_hbm.at[level, :, mine], lsem.at[6 + level])
         hand = copy(stage_other.at[level], out_hbm.at[level, :, mine], SEM_AT["out"] + level, core)
@@ -442,6 +473,7 @@
         start(reduce_pair("e1", e1s, e1r, ch))
 
     chains(fetch1)
+    chains(back2)
 
     def weigh1(ch):
         carried = summed(reduce_pair("e1", e1s, e1r, ch), e1s[ch, xpar, z], e1r, ch)
@@ -481,30 +513,25 @@
         start(reduce_z("l0", l0s, l0r, ch))
 
     chains(weigh0)
-    finish(1, "d1z", d1zs, d1zr)
-
-    sent(swaps + blocks + hands + t_z + t_x + r1_x + r1_z + r2_z)
-
-    def all_sent(ch):
-        sent(gather_r0(ch))
-        sent(gather_z("a1", s0b, a1r, ch))
-        sent(gather_pair("u0", u0b, u0r, ch))
-        sent(gather_pair("s1", s1b, s1r, ch))
-        sent(gather_skip("u1", u1b, u1r, ch))
-        sent(reduce_x("s2r", s2rs, s2rr, ch))
-        sent(gather_x("s2a", s2b, s2ar, ch))
+
+    def sent_adjoint(ch):
         sent(reduce_skip("f1", f1s, f1r, ch))
         sent(reduce_z("d2z", d2zs, d2zr, ch))
         sent(reduce_pair("e1", e1s, e1r, ch))
         sent(reduce_pair("f0", f0s, f0r, ch))
         sent(x_pair("d1x", d1xs, d1xr, ch))
+        sent(reduce_z("w0", w0s, w0r, ch))
+
+    chains(sent_adjoint)
+    finish(1, "d1z", d1zs, d1zr)
+
+    finish(0, "l0", l0s, l0r)
+
+    def sent_last(ch):
         sent(reduce_z("d1z", d1zs, d1zr, ch))
-        sent(reduce_z("w0", w0s, w0r, ch))
-
-    chains(all_sent)
-
-    finish(0, "l0", l0s, l0r)
-    chains(lambda ch: sent(reduce_z("l0", l0s, l0r, ch)))
+        sent(reduce_z("l0", l0s, l0r, ch))
+
+    chains(sent_last)
     for level in range(3):
         keep, hand = out_copies(level)
         keep.wait()
@@ -513,15 +540,16 @@
 
 def shards(rhs, inverse_blocks, update_blocks, asm_owner, asm_row):
     k, w = CHAINS, WIDTH
-    vmem = pl.BlockSpec(memory_space=pltpu.VMEM)
     hbm = pl.BlockSpec(memory_space=pl.ANY)
     block = lambda *lead: pltpu.VMEM((k, *lead, w, UNIT), BF16)
     return pl.pallas_call(
         kernel,
         out_shape=jax.ShapeDtypeStruct(rhs.shape, F32),
-        in_specs=[vmem, vmem, hbm, hbm, hbm],
+        in_specs=[hbm] * 5,
         out_specs=hbm,
         scratch_shapes=[
+            pltpu.VMEM((2, 1, ROW), jnp.int32),
+            pltpu.VMEM((2, ROW), jnp.int32),
             pltpu.VMEM((3, ROW, 2 * HALF), BF16),
             pltpu.VMEM((UNIT, 3 * LEAF), BF16),
             pltpu.VMEM((LEAF, LEAF), BF16),
@@ -535,7 +563,8 @@
             pltpu.VMEM((NZ, HALF, UNIT), BF16),
             pltpu.VMEM((LEAF, UNIT), BF16),
             block(), block(), block(), block(), block(), block(),
-            block(3), block(3), block(7), block(7), block(7),
+            pltpu.VMEM((NZ, HALF, UNIT), BF16),
+            block(3), block(7), block(7), block(7),
             pltpu.VMEM((k, w, UNIT), F32),
             pltpu.VMEM((k, w, LEAF), F32),
             block(4), block(3), block(3),
@@ -548,10 +577,10 @@
             pltpu.VMEM((3, ROW, HALF), F32),
             pltpu.SemaphoreType.DMA((SEM_COUNT,)),
             pltpu.SemaphoreType.DMA((SEM_COUNT,)),
-            pltpu.SemaphoreType.DMA((9,)),
+            pltpu.SemaphoreType.DMA((13,)),
         ],
-        compiler_params=pltpu.CompilerParams(collective_id=0, has_side_effects=True, vmem_limit_bytes=56 * 2**20),
-    )(asm_owner.reshape(asm_row.shape[0], 1, asm_row.shape[1]), asm_row, rhs, inverse_blocks, update_blocks)
+        compiler_params=pltpu.CompilerParams(collective_id=0, has_side_effects=True, vmem_limit_bytes=32 * 2**20),
+    )(*[pltpu.with_memory_space_constraint(one, pltpu.HBM) for one in (asm_owner.reshape(asm_row.shape[0], 1, asm_row.shape[1]), asm_row, rhs, inverse_blocks, update_blocks)])
 
 
 def solution(mesh):

time: 95.5 us -> 90.8 us (0.951)
  Pallas kernels: 93.6 us -> 89.9 us
  local copies, waits for them, and re-layouts: 1.77 us -> 0.75 us
    pallas_call x1, Pallas kernels: 93.6 us -> 89.9 us  [shards(): pl.pallas_call(kernel, out_shape=jax.ShapeDtypeStruct(rhs.shape, F32), in...]
    unnamed x1, local copies, waits for them, and re-layouts: 1.77 us -> 0.75 us
where the time goes in v3:
time: 90.8 us; the launch traced here: 90.7 us
  Pallas kernels  89.9 us (99%)
    pallas_call x1, Pallas kernels, shards(): pl.pallas_call(kernel, out_shape=jax.ShapeDtypeStruct(rhs.shape, F32), in...  89.9 us

profile of v3, /device:TPU:1, one launch (start us, length us, event | category | flops | bytes accessed | tf_op | source)
XLA Modules:
  0.0 90.7 jit_solution(7589743186776212410)
XLA Ops:
  0.0 89.9 %shard_map.55 = f32[3,128,256]{2,1,0:T(8,128)S(1)} custom-call(s32[2,1,128]{2,1,0:T(1,128)} %bitcast.1, s32[2,128]{1,0:T(2,128)} %row_hbm.1, bf16[3,128,256]{2,1,0:T(8,128)(2,1)} %rhs_hbm.1, bf16[128,7168]{1,0:T(8,128)(2,1)} %d_hbm.1, bf16[128,3072]{1,0:T(8,128)(2,1)} %e_hbm.1), custom_call_target="tpu_custom_call" | custom-call | tf_op jit(solution)/shard_map/pallas_call | solution.py:545
  89.9 0.7 copy.7

commit v4 on v3

--- a/solution.py
+++ b/solution.py
@@ -241,7 +241,7 @@
     start(t_z)
     swaps[1].wait_recv()
     start(r1_x)
-    start(blocks)
+    start(blocks[1:])
     zr1[0, 0] = rt[1]
 
     def d_block(level, index):
@@ -266,6 +266,7 @@
     swaps[0].wait_recv()
     received(r0_same + r0_cross)
     chains(solve0)
+    start(blocks[:1])
 
     received(t_z)
     start(t_x)
@@ -473,7 +474,6 @@
         start(reduce_pair("e1", e1s, e1r, ch))
 
     chains(fetch1)
-    chains(back2)
 
     def weigh1(ch):
         carried = summed(reduce_pair("e1", e1s, e1r, ch), e1s[ch, xpar, z], e1r, ch)
@@ -483,13 +483,13 @@
         start(reduce_pair("f0", f0s, f0r, ch))
 
     chains(weigh1)
+    chains(back2)
 
     def back1(ch):
         spread(dm, D_AT[1], w1b[ch], d1xs, ch, 2)
         start(x_pair("d1x", d1xs, d1xr, ch))
 
     chains(back1)
-    finish(2, "d2z", d2zs, d2zr)
 
     def fetch0(ch):
         fetched = summed(reduce_pair("f0", f0s, f0r, ch), f0s[ch, xpar, z], f0r, ch).astype(BF16)
@@ -497,6 +497,7 @@
         start(reduce_z("w0", w0s, w0r, ch))
 
     chains(fetch0)
+    finish(2, "d2z", d2zs, d2zr)
 
     def back1z(ch):
         received(x_pair("d1x", d1xs, d1xr, ch))

time: 90.8 us -> 89.9 us (0.990)
  no operation moved by 1% of the time
where the time goes in v4:
time: 89.9 us; the launch traced here: 89.8 us
  Pallas kernels  89.1 us (99%)
    pallas_call x1, Pallas kernels, shards(): pl.pallas_call(kernel, out_shape=jax.ShapeDtypeStruct(rhs.shape, F32), in...  89.1 us

profile of v4, /device:TPU:1, one launch (start us, length us, event | category | flops | bytes accessed | tf_op | source)
XLA Modules:
  0.0 89.8 jit_solution(18005772152768537315)
XLA Ops:
  0.0 89.1 %shard_map.55 = f32[3,128,256]{2,1,0:T(8,128)S(1)} custom-call(s32[2,1,128]{2,1,0:T(1,128)} %bitcast.1, s32[2,128]{1,0:T(2,128)} %row_hbm.1, bf16[3,128,256]{2,1,0:T(8,128)(2,1)} %rhs_hbm.1, bf16[128,7168]{1,0:T(8,128)(2,1)} %d_hbm.1, bf16[128,3072]{1,0:T(8,128)(2,1)} %e_hbm.1), custom_call_target="tpu_custom_call" | custom-call | tf_op jit(solution)/shard_map/pallas_call | solution.py:546
  89.1 0.7 copy.7

commit v5 on v4

--- a/solution.py
+++ b/solution.py
@@ -349,7 +349,7 @@
         m2[:, pl.ds(at(j * UNIT), UNIT)] = nn(d2[...], select[...]).astype(BF16)
         return carry
 
-    lax.fori_loop(0, 4, select2, 0)
+    lax.fori_loop(0, 5, select2, 0)
 
     loads[3].wait()
     swaps[7].wait_recv()
@@ -365,7 +365,7 @@
 
     chains(update1)
 
-    lax.fori_loop(4, 8, select2, 0)
+    lax.fori_loop(5, 8, select2, 0)
     received(r2_z)
 
     def rhs2(ch):

time: 89.9 us -> 90.8 us (1.010)
  no operation moved by 1% of the time
where the time goes in v5:
time: 90.8 us; the launch traced here: 90.7 us
  Pallas kernels  89.9 us (99%)
    pallas_call x1, Pallas kernels, shards(): pl.pallas_call(kernel, out_shape=jax.ShapeDtypeStruct(rhs.shape, F32), in...  89.9 us

profile of v5, /device:TPU:1, one launch (start us, length us, event | category | flops | bytes accessed | tf_op | source)
XLA Modules:
  0.0 90.7 jit_solution(14962248272794261466)
XLA Ops:
  0.0 89.9 %shard_map.55 = f32[3,128,256]{2,1,0:T(8,128)S(1)} custom-call(s32[2,1,128]{2,1,0:T(1,128)} %bitcast.1, s32[2,128]{1,0:T(2,128)} %row_hbm.1, bf16[3,128,256]{2,1,0:T(8,128)(2,1)} %rhs_hbm.1, bf16[128,7168]{1,0:T(8,128)(2,1)} %d_hbm.1, bf16[128,3072]{1,0:T(8,128)(2,1)} %e_hbm.1), custom_call_target="tpu_custom_call" | custom-call | tf_op jit(solution)/shard_map/pallas_call | solution.py:546
  89.9 0.7 copy.7
